TPU v7x, 512 devices: a whole 4x4x16 slice. The times are simulated.
512 devices in a mesh: af: 8 (over x, z_hi), vert: 64 (over y, z_lo, core).
Axes of the slice: x: 4, y: 4, z: 16 (z_hi: 2, z_lo: 8; z = z_hi * 8 + z_lo), core: 2. Of those that a mesh axis runs over, the one named last changes fastest.
Arguments:
- signals: bfloat16 [1000, 16384], P('af', 'vert'), may hold values from -2000 to 2000
- basis: bfloat16 [10, 1000], P(None, 'af'), may hold values from -0.1875 to 0.1875
- atoms: float32 [10, 262144], P(None, ('af', 'vert')), may hold values from -6 to 6
- params: float32 [3, 262144], P(None, ('af', 'vert')), may hold values from -1.5 to 1.5
Outputs:
- coefficients: float32 [10, 16384], P(None, 'vert')
- maps: float32 [3, 16384], P(None, 'vert')
All inputs are finite; a program needn't handle non-finite values.
Results may differ from a plain program's by a relative error of at most 0.0003.
Values sent between devices are 32-bit elements; how exact they have to be, the bound alone decides.
No kernel may reach another device: no remote copies, remote signals or barrier semaphores. Data moves between devices by JAX's collectives and lax.ppermute only.
A program may use at most 64 MiB of HBM per device.

v0:
```python
import math

import jax
import jax.numpy as jnp
from jax import lax
from jax.experimental import pallas as pl
from jax.experimental.pallas import tpu as pltpu
from jax.sharding import Mesh
from jax.sharding import PartitionSpec as P


scale = 1.5 * math.log2(math.e)
limit = 2.0**100

ATOM_ROWS, ONE_ROW, ROWS = 10, 13, 16


def split(values):
    high = values.astype(jnp.bfloat16)
    rest = values - high.astype(jnp.float32)
    middle = rest.astype(jnp.bfloat16)
    low = (rest - middle.astype(jnp.float32)).astype(jnp.bfloat16)
    return high, middle, low


def unpack_kernel(coefs_ref, plain_ref, own_coefs_ref):
    groups = coefs_ref.shape[0] // 2
    half = coefs_ref.shape[2]
    mine = lax.axis_index("zl")
    mine_sum = coefs_ref[mine] + coefs_ref[groups + mine]
    own_coefs_ref[:, :half] = mine_sum[:ATOM_ROWS]
    own_coefs_ref[:, half:] = mine_sum[ATOM_ROWS:]

    zeros = jnp.zeros((ROWS - ATOM_ROWS, half), jnp.float32)
    for g in range(groups):
        both = scale * (coefs_ref[g] + coefs_ref[groups + g])
        for h in range(2):
            part = both[h * ATOM_ROWS : (h + 1) * ATOM_ROWS]
            at = (2 * g + h) * half
            plain_ref[:, at : at + half] = jnp.concatenate([part, zeros], axis=0)


def match_kernel(plain, own_ref, core_ref, near_ref, far_ref, state_ref, shifted, sums, peak):
    groups = state_ref.shape[0] // 2
    width = state_ref.shape[2]
    row = lax.broadcasted_iota(jnp.int32, (ROWS, 1), 0)

    def stack(values):
        high, middle, low = split(values)
        return jnp.concatenate([high, middle, low, high, middle, high], axis=0)

    def atom_terms(piece):
        high, middle, low = split(piece)
        return jnp.concatenate([high, high, high, middle, middle, low], axis=0)

    def param_terms(piece):
        kept = jnp.where((row >= ATOM_ROWS) & (row <= ONE_ROW), piece, 0.0)
        high, middle, low = split(kept)
        rolled = (
            high.astype(jnp.float32)
            + pltpu.roll(middle.astype(jnp.float32), 6, 0)
            + pltpu.roll(low.astype(jnp.float32), 10, 0)
        )
        return rolled.astype(jnp.bfloat16)

    def scores_of(terms, stacked):
        return lax.dot_general(terms, stacked, (((0,), (0,)), ((), ())), preferred_element_type=jnp.float32)

    def weigh(params, weights):
        high = weights.astype(jnp.bfloat16)
        low = (weights - high.astype(jnp.float32)).astype(jnp.bfloat16)
        return jnp.dot(params, high, preferred_element_type=jnp.float32) + jnp.dot(
            params, low, preferred_element_type=jnp.float32
        )

    peak[...] = jnp.max(scores_of(atom_terms(own_ref[0]), stack(plain[...])), axis=0, keepdims=True)
    shifted[...] = stack(jnp.where(row == ONE_ROW, -peak[...], plain[...]))
    sums[...] = jnp.zeros_like(sums)

    def fast(pieces, i):
        piece = pieces[i]
        sums[...] += weigh(param_terms(piece), jnp.exp2(scores_of(atom_terms(piece), shifted[...])))

    def careful(pieces, i):
        piece = pieces[i]
        scores = scores_of(atom_terms(piece), stack(plain[...]))
        top = jnp.maximum(peak[...], jnp.max(scores, axis=0, keepdims=True))
        sums[...] = sums[...] * jnp.exp2(peak[...] - top) + weigh(param_terms(piece), jnp.exp2(scores - top))
        peak[...] = top

    def over_pieces(step):
        for pieces in (own_ref, core_ref, near_ref, far_ref):
            count = pieces.shape[0]
            if count == 1:
                step(pieces, 0)
            else:
                lax.fori_loop(0, count, lambda i, _, pieces=pieces: (step(pieces, i), 0)[1], 0)

    over_pieces(fast)

    fine = jnp.all(sums[ONE_ROW : ONE_ROW + 1, :] < limit)

    @pl.when(jnp.logical_not(fine))
    def _():
        sums[...] = jnp.zeros_like(sums)
        over_pieces(careful)

    total = sums[ONE_ROW : ONE_ROW + 1, :]
    weighted = sums[10:13, :] + sums[0:3, :] + sums[4:7, :]
    for g in range(groups):
        at = slice(g * width, (g + 1) * width)
        state = jnp.concatenate([peak[:, at], total[:, at], weighted[:, at], jnp.zeros((3, width), jnp.float32)], axis=0)
        state_ref[g] = state
        state_ref[groups + g] = state


def match(plain, own, core, near, far, groups):
    everything = plain.shape[1]
    return pl.pallas_call(
        match_kernel,
        out_shape=shape(2 * groups, 8, everything // groups),
        in_specs=[pl.BlockSpec(memory_space=pltpu.VMEM)] * 5,
        out_specs=pl.BlockSpec(memory_space=pltpu.VMEM),
        scratch_shapes=[
            pltpu.VMEM((6 * ROWS, everything), jnp.bfloat16),
            pltpu.VMEM((ROWS, everything), jnp.float32),
            pltpu.VMEM((1, everything), jnp.float32),
        ],
        compiler_params=pltpu.CompilerParams(vmem_limit_bytes=24 << 20),
        name="match",
    )(plain, own, core, near, far)


def call(kernel, shapes, *arrays):
    return pl.pallas_call(
        kernel,
        out_shape=shapes,
        in_specs=[pl.BlockSpec(memory_space=pltpu.VMEM)] * len(arrays),
        out_specs=jax.tree.map(lambda _: pl.BlockSpec(memory_space=pltpu.VMEM), shapes),
        compiler_params=pltpu.CompilerParams(vmem_limit_bytes=4 << 20),
    )(*arrays)


def pack_kernel(atoms_ref, params_ref, own_ref):
    own_ref[0, :ATOM_ROWS] = atoms_ref[...]
    own_ref[0, ATOM_ROWS:ONE_ROW] = params_ref[...]
    own_ref[0, ONE_ROW : ONE_ROW + 1] = jnp.ones((1, atoms_ref.shape[1]), jnp.float32)
    own_ref[0, ONE_ROW + 1 :] = jnp.zeros((ROWS - ONE_ROW - 1, atoms_ref.shape[1]), jnp.float32)


def project_kernel(basis_ref, signals_ref, out_ref):
    sums = jnp.dot(basis_ref[...], signals_ref[...], preferred_element_type=jnp.float32)
    half = sums.shape[1] // 2
    for i in range(out_ref.shape[0]):
        out_ref[i, :ATOM_ROWS] = sums[:, :half]
        out_ref[i, ATOM_ROWS:] = sums[:, half:]


def add_kernel(parts_ref, out_ref):
    total = jnp.sum(parts_ref[...], axis=0)
    for i in range(out_ref.shape[0]):
        out_ref[i] = total


def merged(states):
    peak = jnp.max(states[:, :1], axis=0)
    return peak, jnp.sum(states * jnp.exp2(states[:, :1] - peak[None]), axis=0)


def merge_kernel(states_ref, out_ref):
    peak, sums = merged(states_ref[...])
    row = lax.broadcasted_iota(jnp.int32, sums.shape, 0)
    state = jnp.where(row == 0, peak, sums)
    for i in range(out_ref.shape[0]):
        out_ref[i] = state


def finish_kernel(states_ref, maps_ref):
    _, sums = merged(states_ref[...])
    maps_ref[...] = sums[2:5] / sums[1:2]


def shape(*sizes):
    return jax.ShapeDtypeStruct(sizes, jnp.float32)


def exchange(array, axis, mask):
    return lax.ppermute(array, axis, [(i, i ^ mask) for i in range(lax.axis_size(axis))])


def on_device(signals, basis, atoms, params):
    width, voxels = atoms.shape[1], signals.shape[1]
    across, along = lax.axis_size("x"), lax.axis_size(("zh", "zl"))
    own = call(pack_kernel, shape(1, ROWS, width), atoms, params)
    core = exchange(own, "c", 1)
    sums = call(project_kernel, shape(across, 2 * ATOM_ROWS, voxels // 2), basis, signals)
    near = exchange(jnp.concatenate([own, core]), "y", 1)
    sums = lax.all_to_all(sums, "x", 0, 0)
    sums = call(add_kernel, shape(along, 2 * ATOM_ROWS, voxels // 2), sums)
    far = exchange(jnp.concatenate([own, core, near]), "y", 2)
    coefs = lax.all_to_all(sums, ("zh", "zl"), 0, 0)

    groups = along // 2
    plain, coefficients = call(unpack_kernel, (shape(ROWS, groups * voxels), shape(ATOM_ROWS, voxels)), coefs)
    states = match(plain, own, core, near, far, groups)
    states = lax.all_to_all(states, ("zh", "zl"), 0, 0)
    states = call(merge_kernel, shape(across, 8, voxels), states)
    states = lax.all_to_all(states, "x", 0, 0)
    maps = call(finish_kernel, shape(3, voxels), states)
    return coefficients, maps


def solution(mesh):
    sizes = dict(zip(("x", "zh", "y", "zl", "c"), (4, 2, 4, 8, 2)))
    fine = Mesh(mesh.devices.reshape(tuple(sizes.values())), tuple(sizes))
    af, vert = ("x", "zh"), ("y", "zl", "c")
    return jax.shard_map(
        on_device,
        mesh=fine,
        in_specs=(P(af, vert), P(None, af), P(None, af + vert), P(None, af + vert)),
        out_specs=(P(None, vert), P(None, vert)),
        check_vma=False,
    )
```

profile of v0, /device:TPU:8, one launch (start us, length us, event | category | flops | bytes accessed | tf_op | source)
XLA Modules:
  0.0 105.8 jit_solution(7037290611851433661)
XLA Ops:
  0.6 0.0 copy-start
  0.6 0.8 copy-done
  1.5 0.0 copy-start.3
  1.5 0.7 copy-done.3
  2.2 0.1 shard_map.59
  2.3 9.6 %all_to_all.20.parts_ref = f32[4,20,128]{2,1,0:T(8,128)S(1)} all-to-all(f32[4,20,128]{2,1,0:T(8,128)S(1)} %shard_map.59), channel_id=1, replica_groups=mesh['x'=4,'zh'=2,'y'=4,'zl'=8,'c'=2] {'x'}, dimensions={0} | all-to-all | bytes 81920 | tf_op jit(solution)/shard_map/all_to_all | solution.py:198
  11.9 0.7 shard_map.60
  12.6 0.0 copy-start.1
  12.6 0.0 copy-start.2
  12.6 15.3 %all-to-all-start.1 = ((f32[16,20,128]{2,1,0:T(8,128)}), f32[16,20,128]{2,1,0:T(8,128)S(1)}, u32[]{:S(2)}, u32[]{:S(2)}) async-start(f32[16,20,128]{2,1,0:T(8,128)} %shard_map.60), calls=%async_computation.1 | async-start | bytes 393216 | tf_op jit(solution)/shard_map/all_to_all | solution.py:201
  27.9 0.0 copy-done.1
  28.0 0.0 copy-done.2
  28.0 1.9 %collective-permute-start = (f32[1,16,512]{2,1,0:T(8,128)S(1)}, f32[1,16,512]{2,1,0:T(8,128)S(1)}, u32[]{:S(2)}, u32[]{:S(2)}) collective-permute-start(f32[1,16,512]{2,1,0:T(8,128)S(1)} %shard_map.62.own_ref), channel_id=1, source_target_pairs={{0,1},{1,0},{2,3},{3,2},{4,5},{5,4},{6,7},{7,6},{8,9},{9,8},{10,11... | collective-permute-start | bytes 98312 | tf_op jit(solution)/shard_map/ppermute | solution.py:188
  29.9 1.2 %collective-permute-done.core_ref = f32[1,16,512]{2,1,0:T(8,128)S(1)} collective-permute-done((f32[1,16,512]{2,1,0:T(8,128)S(1)}, f32[1,16,512]{2,1,0:T(8,128)S(1)}, u32[]{:S(2)}, u32[]{:S(2)}) %collective-permute-start) | collective-permute-done | bytes 32800 | tf_op jit(solution)/shard_map/ppermute | solution.py:188
  31.1 2.3 %collective-permute-start.1 = (f32[2,16,512]{2,1,0:T(8,128)S(1)}, f32[2,16,512]{2,1,0:T(8,128)S(1)}, u32[]{:S(2)}, u32[]{:S(2)}) collective-permute-start(f32[2,16,512]{2,1,0:T(8,128)S(1)} %pad_maximum_fusion.1), channel_id=1, source_target_pairs={{0,16},{16,0},{32,48},{48,32},{1,17},{17,1},{33,49},{49,33},{2,18}... | collective-permute-start | bytes 196616 | tf_op jit(solution)/shard_map/ppermute | solution.py:188
  33.4 3.8 %collective-permute-done.1.near_ref = f32[2,16,512]{2,1,0:T(8,128)S(1)} collective-permute-done((f32[2,16,512]{2,1,0:T(8,128)S(1)}, f32[2,16,512]{2,1,0:T(8,128)S(1)}, u32[]{:S(2)}, u32[]{:S(2)}) %collective-permute-start.1) | collective-permute-done | bytes 65568 | tf_op jit(solution)/shard_map/ppermute | solution.py:188
  37.2 4.2 %collective-permute-start.2 = (f32[4,16,512]{2,1,0:T(8,128)S(1)}, f32[4,16,512]{2,1,0:T(8,128)S(1)}, u32[]{:S(2)}, u32[]{:S(2)}) collective-permute-start(f32[4,16,512]{2,1,0:T(8,128)S(1)} %pad_maximum_fusion), channel_id=1, source_target_pairs={{0,32},{16,48},{32,0},{48,16},{1,33},{17,49},{33,1},{49,17},{2,34}... | collective-permute-start | bytes 393224 | tf_op jit(solution)/shard_map/ppermute | solution.py:188
  41.5 2.1 %all-to-all-done.1.coefs_ref = f32[16,20,128]{2,1,0:T(8,128)S(1)} async-done(((f32[16,20,128]{2,1,0:T(8,128)}), f32[16,20,128]{2,1,0:T(8,128)S(1)}, u32[]{:S(2)}, u32[]{:S(2)}) %all-to-all-start.1) | async-done | bytes 163872 | tf_op jit(solution)/shard_map/all_to_all | solution.py:201
  43.5 0.6 shard_map.61
  44.1 1.5 %collective-permute-done.2.far_ref = f32[4,16,512]{2,1,0:T(8,128)S(1)} collective-permute-done((f32[4,16,512]{2,1,0:T(8,128)S(1)}, f32[4,16,512]{2,1,0:T(8,128)S(1)}, u32[]{:S(2)}, u32[]{:S(2)}) %collective-permute-start.2) | collective-permute-done | bytes 131104 | tf_op jit(solution)/shard_map/ppermute | solution.py:188
  45.6 26.6 %match.1 = f32[16,8,256]{2,1,0:T(8,128)S(1)} custom-call(f32[16,2048]{1,0:T(8,128)S(1)} %get-tuple-element.5.plain, f32[1,16,512]{2,1,0:T(8,128)S(1)} %shard_map.62.own_ref, f32[1,16,512]{2,1,0:T(8,128)S(1)} %collective-permute-done.core_ref, f32[2,16,512]{2,1,0:T(8,128)S(1)} %collective-permute-done.1.near_ref, f32[4,16,512]{2,1,0:T(8,128)S(1)} %collective-permute-done.2.far_ref), custom_call_target="tpu_custom_call" | custom-call | tf_op jit(solution)/shard_map/match/pallas_call | solution.py:119
  72.2 25.1 %all_to_all.21.states_ref = f32[16,8,256]{2,1,0:T(8,128)S(1)} all-to-all(f32[16,8,256]{2,1,0:T(8,128)S(1)} %match.1), channel_id=1, replica_groups=mesh['x'=4,'zh'=2,'y'=4,'zl'=8,'c'=2] {'zh','zl'}, dimensions={0} | all-to-all | bytes 262144 | tf_op jit(solution)/shard_map/all_to_all | solution.py:206
  97.3 7.8 %all_to_all.22.states_ref = f32[4,8,256]{2,1,0:T(8,128)S(1)} all-to-all(f32[4,8,256]{2,1,0:T(8,128)S(1)} %shard_map.63), channel_id=1, replica_groups=mesh['x'=4,'zh'=2,'y'=4,'zl'=8,'c'=2] {'x'}, dimensions={0} | all-to-all | bytes 65536 | tf_op jit(solution)/shard_map/all_to_all | solution.py:208
  105.1 0.6 shard_map.64
  (4 shorter events, 0.1 us)
Async XLA Ops:
  0.6 0.8 copy-start
  1.5 0.7 copy-start.3
  12.6 15.3 %copy-start.1 = (f32[10,512]{1,0:T(8,128)S(1)}, f32[10,512]{1,0:T(8,128)}, u32[]{:S(2)}) copy-start(f32[10,512]{1,0:T(8,128)} %atoms_ref.1) | copy-start | bytes 61444
  12.6 15.3 %copy-start.2 = (f32[3,512]{1,0:T(4,128)S(1)}, f32[3,512]{1,0:T(4,128)}, u32[]{:S(2)}) copy-start(f32[3,512]{1,0:T(4,128)} %params_ref.1) | copy-start | bytes 18436
  12.6 30.9 %all-to-all-start.1 = ((f32[16,20,128]{2,1,0:T(8,128)}), f32[16,20,128]{2,1,0:T(8,128)S(1)}, u32[]{:S(2)}, u32[]{:S(2)}) async-start(f32[16,20,128]{2,1,0:T(8,128)} %shard_map.60), calls=%async_computation.1 | async-start | bytes 393216 | tf_op jit(solution)/shard_map/all_to_all | solution.py:201
  28.0 3.1 %collective-permute-start = (f32[1,16,512]{2,1,0:T(8,128)S(1)}, f32[1,16,512]{2,1,0:T(8,128)S(1)}, u32[]{:S(2)}, u32[]{:S(2)}) collective-permute-start(f32[1,16,512]{2,1,0:T(8,128)S(1)} %shard_map.62.own_ref), channel_id=1, source_target_pairs={{0,1},{1,0},{2,3},{3,2},{4,5},{5,4},{6,7},{7,6},{8,9},{9,8},{10,11... | collective-permute-start | bytes 98312 | tf_op jit(solution)/shard_map/ppermute | solution.py:188
  31.1 6.1 %collective-permute-start.1 = (f32[2,16,512]{2,1,0:T(8,128)S(1)}, f32[2,16,512]{2,1,0:T(8,128)S(1)}, u32[]{:S(2)}, u32[]{:S(2)}) collective-permute-start(f32[2,16,512]{2,1,0:T(8,128)S(1)} %pad_maximum_fusion.1), channel_id=1, source_target_pairs={{0,16},{16,0},{32,48},{48,32},{1,17},{17,1},{33,49},{49,33},{2,18}... | collective-permute-start | bytes 196616 | tf_op jit(solution)/shard_map/ppermute | solution.py:188
  37.2 8.4 %collective-permute-start.2 = (f32[4,16,512]{2,1,0:T(8,128)S(1)}, f32[4,16,512]{2,1,0:T(8,128)S(1)}, u32[]{:S(2)}, u32[]{:S(2)}) collective-permute-start(f32[4,16,512]{2,1,0:T(8,128)S(1)} %pad_maximum_fusion), channel_id=1, source_target_pairs={{0,32},{16,48},{32,0},{48,16},{1,33},{17,49},{33,1},{49,17},{2,34}... | collective-permute-start | bytes 393224 | tf_op jit(solution)/shard_map/ppermute | solution.py:188
where the time goes:
time: 106 us
  blocking collectives  42.5 us (40%)
  Pallas kernels  28.7 us (27%)
  starting transfers between devices  23.8 us (22%)
  waiting for transfers between devices  8.5 us (8%)
  local copies, waits for them, and re-layouts  1.53 us (1%)
    pallas_call x1, Pallas kernels, match(): pl.pallas_call(match_kernel, out_shape=shape(2 * groups, 8, everything //...  26.6 us
    all_to_all x1, blocking collectives, on_device(): states = lax.all_to_all(states, ('zh', 'zl'), 0, 0)  25.1 us
    all_to_all x1, starting transfers between devices, on_device(): coefs = lax.all_to_all(sums, ('zh', 'zl'), 0, 0)  15.3 us
    all_to_all x1, blocking collectives, on_device(): sums = lax.all_to_all(sums, 'x', 0, 0)  9.63 us
    ppermute x3, starting transfers between devices, exchange(): lax.ppermute(array, axis, [(i, i ^ mask) for i in range(lax.axis_size(axi...  8.47 us
    all_to_all x1, blocking collectives, on_device(): states = lax.all_to_all(states, 'x', 0, 0)  7.8 us
    ppermute x3, waiting for transfers between devices, exchange(): lax.ppermute(array, axis, [(i, i ^ mask) for i in range(lax.axis_size(axi...  6.44 us
  transfers between devices with their start and end apart: 4, of which 4 were waited for; matrix products, arithmetic and copies ran while one was open for 0% of the time, Pallas kernels for 1%

commit v1 on v0

v1 whole, which is shorter than its diff:
```python
import math

import jax
import jax.numpy as jnp
from jax import lax
from jax.experimental import pallas as pl
from jax.experimental.pallas import tpu as pltpu
from jax.sharding import Mesh
from jax.sharding import PartitionSpec as P


scale = 1.5 * math.log2(math.e)
limit = 2.0**100

ATOM_ROWS, ONE_ROW, ROWS = 10, 13, 16


def split(values):
    high = values.astype(jnp.bfloat16)
    rest = values - high.astype(jnp.float32)
    middle = rest.astype(jnp.bfloat16)
    low = (rest - middle.astype(jnp.float32)).astype(jnp.bfloat16)
    return high, middle, low


def stack(values):
    high, middle, low = split(values)
    return jnp.concatenate([high, middle, low, high, middle, high], axis=0)


def atom_terms(piece):
    high, middle, low = split(piece)
    return jnp.concatenate([high, high, high, middle, middle, low], axis=0)


def row_index():
    return lax.broadcasted_iota(jnp.int32, (ROWS, 1), 0)


def param_terms(piece):
    row = row_index()
    kept = jnp.where((row >= ATOM_ROWS) & (row <= ONE_ROW), piece, 0.0)
    high, middle, low = split(kept)
    rolled = (
        high.astype(jnp.float32)
        + pltpu.roll(middle.astype(jnp.float32), 6, 0)
        + pltpu.roll(low.astype(jnp.float32), 10, 0)
    )
    return rolled.astype(jnp.bfloat16)


def scores_of(terms, stacked):
    return lax.dot_general(terms, stacked, (((0,), (0,)), ((), ())), preferred_element_type=jnp.float32)


def weigh(params, weights):
    high = weights.astype(jnp.bfloat16)
    low = (weights - high.astype(jnp.float32)).astype(jnp.bfloat16)
    return jnp.dot(params, high, preferred_element_type=jnp.float32) + jnp.dot(
        params, low, preferred_element_type=jnp.float32
    )


def over_pieces(refs, step):
    for pieces in refs:
        count = pieces.shape[0]
        if count == 1:
            step(pieces, 0)
        else:
            lax.fori_loop(0, count, lambda i, _, pieces=pieces: (step(pieces, i), 0)[1], 0)


def add_weights(refs, shifted, sums):
    def step(pieces, i):
        piece = pieces[i]
        sums[...] += weigh(param_terms(piece), jnp.exp2(scores_of(atom_terms(piece), shifted[...])))

    over_pieces(refs, step)


def begin_kernel(coefs_ref, own_ref, core_ref, near_ref, plain, shifted, peak, sums, own_coefs_ref, kept, sem):
    groups = coefs_ref.shape[0] // 2
    half = coefs_ref.shape[2]
    mine = lax.axis_index("zl")
    mine_sum = coefs_ref[mine] + coefs_ref[groups + mine]
    kept[:, :half] = mine_sum[:ATOM_ROWS]
    kept[:, half:] = mine_sum[ATOM_ROWS:]
    copy = pltpu.make_async_copy(kept, own_coefs_ref, sem)
    copy.start()

    zeros = jnp.zeros((ROWS - ATOM_ROWS, half), jnp.float32)
    for g in range(groups):
        both = scale * (coefs_ref[g] + coefs_ref[groups + g])
        for h in range(2):
            part = both[h * ATOM_ROWS : (h + 1) * ATOM_ROWS]
            at = (2 * g + h) * half
            plain[:, at : at + half] = jnp.concatenate([part, zeros], axis=0)

    peak[...] = jnp.max(scores_of(atom_terms(own_ref[0]), stack(plain[...])), axis=0, keepdims=True)
    shifted[...] = stack(jnp.where(row_index() == ONE_ROW, -peak[...], plain[...]))
    sums[...] = jnp.zeros_like(sums)
    add_weights((own_ref, core_ref, near_ref), shifted, sums)
    copy.wait()


def end_kernel(plain, shifted, first_peak, first_sums, own_ref, core_ref, near_ref, far_ref, state_ref, peak, sums):
    groups = state_ref.shape[0] // 2
    width = state_ref.shape[2]
    peak[...] = first_peak[...]
    sums[...] = first_sums[...]
    add_weights((far_ref,), shifted, sums)
    fine = jnp.all(sums[ONE_ROW : ONE_ROW + 1, :] < limit)

    @pl.when(jnp.logical_not(fine))
    def _():
        sums[...] = jnp.zeros_like(sums)

        def step(pieces, i):
            piece = pieces[i]
            scores = scores_of(atom_terms(piece), stack(plain[...]))
            top = jnp.maximum(peak[...], jnp.max(scores, axis=0, keepdims=True))
            sums[...] = sums[...] * jnp.exp2(peak[...] - top) + weigh(param_terms(piece), jnp.exp2(scores - top))
            peak[...] = top

        over_pieces((own_ref, core_ref, near_ref, far_ref), step)

    total = sums[ONE_ROW : ONE_ROW + 1, :]
    weighted = sums[10:13, :] + sums[0:3, :] + sums[4:7, :]
    for g in range(groups):
        at = slice(g * width, (g + 1) * width)
        state = jnp.concatenate([peak[:, at], total[:, at], weighted[:, at], jnp.zeros((3, width), jnp.float32)], axis=0)
        state_ref[g] = state
        state_ref[groups + g] = state


def in_vmem():
    return pl.BlockSpec(memory_space=pltpu.VMEM)


def begin(coefs, own, core, near):
    groups, voxels = coefs.shape[0] // 2, 2 * coefs.shape[2]
    everything = groups * voxels
    return pl.pallas_call(
        begin_kernel,
        out_shape=(
            shape(ROWS, everything),
            jax.ShapeDtypeStruct((6 * ROWS, everything), jnp.bfloat16),
            shape(1, everything),
            shape(ROWS, everything),
            shape(ATOM_ROWS, voxels),
        ),
        in_specs=[in_vmem()] * 4,
        out_specs=(in_vmem(),) * 4 + (pl.BlockSpec(memory_space=pl.ANY),),
        scratch_shapes=[pltpu.VMEM((ATOM_ROWS, voxels), jnp.float32), pltpu.SemaphoreType.DMA],
        compiler_params=pltpu.CompilerParams(vmem_limit_bytes=24 << 20),
        name="begin",
    )(coefs, own, core, near)


def end(groups, plain, *rest):
    everything = plain.shape[1]
    return pl.pallas_call(
        end_kernel,
        out_shape=shape(2 * groups, 8, everything // groups),
        in_specs=[in_vmem()] * 8,
        out_specs=in_vmem(),
        scratch_shapes=[pltpu.VMEM((1, everything), jnp.float32), pltpu.VMEM((ROWS, everything), jnp.float32)],
        compiler_params=pltpu.CompilerParams(vmem_limit_bytes=24 << 20),
        name="end",
    )(plain, *rest)


def call(kernel, shapes, *arrays):
    return pl.pallas_call(
        kernel,
        out_shape=shapes,
        in_specs=[pl.BlockSpec(memory_space=pltpu.VMEM)] * len(arrays),
        out_specs=jax.tree.map(lambda _: pl.BlockSpec(memory_space=pltpu.VMEM), shapes),
        compiler_params=pltpu.CompilerParams(vmem_limit_bytes=4 << 20),
    )(*arrays)


def pack_kernel(atoms_ref, params_ref, own_ref):
    own_ref[0, :ATOM_ROWS] = atoms_ref[...]
    own_ref[0, ATOM_ROWS:ONE_ROW] = params_ref[...]
    own_ref[0, ONE_ROW : ONE_ROW + 1] = jnp.ones((1, atoms_ref.shape[1]), jnp.float32)
    own_ref[0, ONE_ROW + 1 :] = jnp.zeros((ROWS - ONE_ROW - 1, atoms_ref.shape[1]), jnp.float32)


def project_kernel(basis_ref, signals_ref, out_ref):
    sums = jnp.dot(basis_ref[...], signals_ref[...], preferred_element_type=jnp.float32)
    half = sums.shape[1] // 2
    for i in range(out_ref.shape[0]):
        out_ref[i, :ATOM_ROWS] = sums[:, :half]
        out_ref[i, ATOM_ROWS:] = sums[:, half:]


def add_kernel(parts_ref, out_ref):
    total = jnp.sum(parts_ref[...], axis=0)
    for i in range(out_ref.shape[0]):
        out_ref[i] = total


def merged(states):
    peak = jnp.max(states[:, :1], axis=0)
    return peak, jnp.sum(states * jnp.exp2(states[:, :1] - peak[None]), axis=0)


def merge_kernel(states_ref, out_ref):
    peak, sums = merged(states_ref[...])
    row = lax.broadcasted_iota(jnp.int32, sums.shape, 0)
    state = jnp.where(row == 0, peak, sums)
    for i in range(out_ref.shape[0]):
        out_ref[i] = state


def finish_kernel(states_ref, maps_ref):
    _, sums = merged(states_ref[...])
    maps_ref[...] = sums[2:5] / sums[1:2]


def shape(*sizes):
    return jax.ShapeDtypeStruct(sizes, jnp.float32)


def exchange(array, axis, mask):
    return lax.ppermute(array, axis, [(i, i ^ mask) for i in range(lax.axis_size(axis))])


def on_device(signals, basis, atoms, params):
    width, voxels = atoms.shape[1], signals.shape[1]
    across, along = lax.axis_size("x"), lax.axis_size(("zh", "zl"))
    sums = call(project_kernel, shape(across, 2 * ATOM_ROWS, voxels // 2), basis, signals)
    own = call(pack_kernel, shape(1, ROWS, width), atoms, params)
    sums = lax.all_to_all(sums, "x", 0, 0)
    core = exchange(own, "c", 1)
    sums = call(add_kernel, shape(along, 2 * ATOM_ROWS, voxels // 2), sums)
    coefs = lax.all_to_all(sums, ("zh", "zl"), 0, 0)
    near = exchange(jnp.concatenate([own, core]), "y", 1)
    far = exchange(jnp.concatenate([own, core, near]), "y", 2)

    groups = along // 2
    plain, shifted, peak, sums, coefficients = begin(coefs, own, core, near)
    states = end(groups, plain, shifted, peak, sums, own, core, near, far)
    states = lax.all_to_all(states, ("zh", "zl"), 0, 0)
    states = call(merge_kernel, shape(across, 8, voxels), states)
    states = lax.all_to_all(states, "x", 0, 0)
    maps = call(finish_kernel, shape(3, voxels), states)
    return coefficients, maps


def solution(mesh):
    sizes = dict(zip(("x", "zh", "y", "zl", "c"), (4, 2, 4, 8, 2)))
    fine = Mesh(mesh.devices.reshape(tuple(sizes.values())), tuple(sizes))
    af, vert = ("x", "zh"), ("y", "zl", "c")
    return jax.shard_map(
        on_device,
        mesh=fine,
        in_specs=(P(af, vert), P(None, af), P(None, af + vert), P(None, af + vert)),
        out_specs=(P(None, vert), P(None, vert)),
        check_vma=False,
    )
```

time: 106 us -> 103 us (0.972)
  waiting for transfers between devices: 8.5 us -> 7.03 us
  blocking collectives: 42.5 us -> 41.1 us
    ppermute x3, waiting for transfers between devices: 6.44 us -> 4.97 us  [exchange(): lax.ppermute(array, axis, [(i, i ^ mask) for i in range(lax.axis_size(axi...]
    all_to_all x1, blocking collectives: 25.1 us -> 23.7 us  [on_device(): states = lax.all_to_all(states, ('zh', 'zl'), 0, 0)]
    pallas_call x1 -> x2, Pallas kernels: 26.6 us -> 26.7 us  [the longest x1 21 us: end(): pl.pallas_call(end_kernel, out_shape=shape(2 * groups, 8, everything // g...]
  transfers between devices with their start and end apart: 4 -> 4, of which waited for: 4 -> 3; matrix products, arithmetic and copies ran while one was open for 0% -> 0% of each run, Pallas kernels for 1% -> 6%
where the time goes in v1:
time: 103 us; the launch traced here: 102 us
  blocking collectives  41.1 us (40%)
  Pallas kernels  28.2 us (27%)
  starting transfers between devices  23.8 us (23%)
  waiting for transfers between devices  7.03 us (7%)
  local copies, waits for them, and re-layouts  1.53 us (1%)
    all_to_all x1, blocking collectives, on_device(): states = lax.all_to_all(states, ('zh', 'zl'), 0, 0)  23.7 us
    pallas_call x1, Pallas kernels, end(): pl.pallas_call(end_kernel, out_shape=shape(2 * groups, 8, everything // g...  21 us
    all_to_all x1, starting transfers between devices, on_device(): coefs = lax.all_to_all(sums, ('zh', 'zl'), 0, 0)  15.3 us
    all_to_all x1, blocking collectives, on_device(): sums = lax.all_to_all(sums, 'x', 0, 0)  9.63 us
    ppermute x3, starting transfers between devices, exchange(): lax.ppermute(array, axis, [(i, i ^ mask) for i in range(lax.axis_size(axi...  8.47 us
    all_to_all x1, blocking collectives, on_device(): states = lax.all_to_all(states, 'x', 0, 0)  7.8 us
    pallas_call x1, Pallas kernels, begin(): pl.pallas_call(begin_kernel, out_shape=(shape(ROWS, everything), jax.Shap...  5.68 us
    ppermute x3, waiting for transfers between devices, exchange(): lax.ppermute(array, axis, [(i, i ^ mask) for i in range(lax.axis_size(axi...  4.97 us
  transfers between devices with their start and end apart: 4, of which 3 were waited for; matrix products, arithmetic and copies ran while one was open for 0% of the time, Pallas kernels for 6%

profile of v1, /device:TPU:8, one launch (start us, length us, event | category | flops | bytes accessed | tf_op | source)
XLA Modules:
  0.0 102.4 jit_solution(14177157556188072465)
XLA Ops:
  0.6 0.0 copy-start
  0.6 0.8 copy-done
  1.5 0.0 copy-start.3
  1.5 0.7 copy-done.3
  2.2 0.1 shard_map.59
  2.3 9.6 %all_to_all.20.parts_ref = f32[4,20,128]{2,1,0:T(8,128)S(1)} all-to-all(f32[4,20,128]{2,1,0:T(8,128)S(1)} %shard_map.59), channel_id=1, replica_groups=mesh['x'=4,'zh'=2,'y'=4,'zl'=8,'c'=2] {'x'}, dimensions={0} | all-to-all | bytes 81920 | tf_op jit(solution)/shard_map/all_to_all | solution.py:235
  11.9 0.7 shard_map.60
  12.6 0.0 copy-start.1
  12.6 0.0 copy-start.2
  12.6 15.3 %all-to-all-start.1 = ((f32[16,20,128]{2,1,0:T(8,128)}), f32[16,20,128]{2,1,0:T(8,128)S(1)}, u32[]{:S(2)}, u32[]{:S(2)}) async-start(f32[16,20,128]{2,1,0:T(8,128)} %shard_map.60), calls=%async_computation.1 | async-start | bytes 393216 | tf_op jit(solution)/shard_map/all_to_all | solution.py:238
  27.9 0.0 copy-done.1
  28.0 0.0 copy-done.2
  28.0 1.9 %collective-permute-start = (f32[1,16,512]{2,1,0:T(8,128)S(1)}, f32[1,16,512]{2,1,0:T(8,128)S(1)}, u32[]{:S(2)}, u32[]{:S(2)}) collective-permute-start(f32[1,16,512]{2,1,0:T(8,128)S(1)} %shard_map.61.own_ref), channel_id=1, source_target_pairs={{0,1},{1,0},{2,3},{3,2},{4,5},{5,4},{6,7},{7,6},{8,9},{9,8},{10,11... | collective-permute-start | bytes 98312 | tf_op jit(solution)/shard_map/ppermute | solution.py:227
  29.9 1.2 %collective-permute-done.core_ref = f32[1,16,512]{2,1,0:T(8,128)S(1)} collective-permute-done((f32[1,16,512]{2,1,0:T(8,128)S(1)}, f32[1,16,512]{2,1,0:T(8,128)S(1)}, u32[]{:S(2)}, u32[]{:S(2)}) %collective-permute-start) | collective-permute-done | bytes 32800 | tf_op jit(solution)/shard_map/ppermute | solution.py:227
  31.1 2.3 %collective-permute-start.1 = (f32[2,16,512]{2,1,0:T(8,128)S(1)}, f32[2,16,512]{2,1,0:T(8,128)S(1)}, u32[]{:S(2)}, u32[]{:S(2)}) collective-permute-start(f32[2,16,512]{2,1,0:T(8,128)S(1)} %pad_maximum_fusion.1), channel_id=1, source_target_pairs={{0,16},{16,0},{32,48},{48,32},{1,17},{17,1},{33,49},{49,33},{2,18}... | collective-permute-start | bytes 196616 | tf_op jit(solution)/shard_map/ppermute | solution.py:227
  33.4 3.8 %collective-permute-done.1.near_ref = f32[2,16,512]{2,1,0:T(8,128)S(1)} collective-permute-done((f32[2,16,512]{2,1,0:T(8,128)S(1)}, f32[2,16,512]{2,1,0:T(8,128)S(1)}, u32[]{:S(2)}, u32[]{:S(2)}) %collective-permute-start.1) | collective-permute-done | bytes 65568 | tf_op jit(solution)/shard_map/ppermute | solution.py:227
  37.2 4.2 %collective-permute-start.2 = (f32[4,16,512]{2,1,0:T(8,128)S(1)}, f32[4,16,512]{2,1,0:T(8,128)S(1)}, u32[]{:S(2)}, u32[]{:S(2)}) collective-permute-start(f32[4,16,512]{2,1,0:T(8,128)S(1)} %pad_maximum_fusion), channel_id=1, source_target_pairs={{0,32},{16,48},{32,0},{48,16},{1,33},{17,49},{33,1},{49,17},{2,34}... | collective-permute-start | bytes 393224 | tf_op jit(solution)/shard_map/ppermute | solution.py:227
  41.5 2.1 %all-to-all-done.1.coefs_ref = f32[16,20,128]{2,1,0:T(8,128)S(1)} async-done(((f32[16,20,128]{2,1,0:T(8,128)}), f32[16,20,128]{2,1,0:T(8,128)S(1)}, u32[]{:S(2)}, u32[]{:S(2)}) %all-to-all-start.1) | async-done | bytes 163872 | tf_op jit(solution)/shard_map/all_to_all | solution.py:238
  43.5 5.7 %begin.1 = (f32[16,2048]{1,0:T(8,128)S(1)}, bf16[96,2048]{1,0:T(8,128)(2,1)S(1)}, f32[1,2048]{1,0:T(1,128)S(1)}, f32[16,2048]{1,0:T(8,128)S(1)}, f32[10,256]{1,0:T(8,128)}) custom-call(f32[16,20,128]{2,1,0:T(8,128)S(1)} %all-to-all-done.1.coefs_ref, f32[1,16,512]{2,1,0:T(8,128)S(1)} %shard_map.61.own_ref, f32[1,16,512]{2,1,0:T(8,128)S(1)} %collective-permute-done.core_ref, ...), custom_call_target="tpu_custom_call" | custom-call | tf_op jit(solution)/shard_map/begin/pallas_call | solution.py:143
  49.2 0.0 collective-permute-done.2.far_ref
  49.2 21.0 %end.1 = f32[16,8,256]{2,1,0:T(8,128)S(1)} custom-call(f32[16,2048]{1,0:T(8,128)S(1)} %get-tuple-element.8.plain, bf16[96,2048]{1,0:T(8,128)(2,1)S(1)} %get-tuple-element.9.shifted, f32[1,2048]{1,0:T(1,128)S(1)} %get-tuple-element.10.first_peak, f32[16,2048]{1,0:T(8,128)S(1)} %get-tuple-element.11.first_sums, f32[1,16,512]{2,1,0:T(8,128)S(1)} %shard_map.61.own_ref, ...), custom_call_target="tpu_custom_call" | custom-call | tf_op jit(solution)/shard_map/end/pallas_call | solution.py:162
  70.2 23.7 %all_to_all.21.states_ref = f32[16,8,256]{2,1,0:T(8,128)S(1)} all-to-all(f32[16,8,256]{2,1,0:T(8,128)S(1)} %end.1), channel_id=1, replica_groups=mesh['x'=4,'zh'=2,'y'=4,'zl'=8,'c'=2] {'zh','zl'}, dimensions={0} | all-to-all | bytes 262144 | tf_op jit(solution)/shard_map/all_to_all | solution.py:245
  94.0 7.8 %all_to_all.22.states_ref = f32[4,8,256]{2,1,0:T(8,128)S(1)} all-to-all(f32[4,8,256]{2,1,0:T(8,128)S(1)} %shard_map.62), channel_id=1, replica_groups=mesh['x'=4,'zh'=2,'y'=4,'zl'=8,'c'=2] {'x'}, dimensions={0} | all-to-all | bytes 65536 | tf_op jit(solution)/shard_map/all_to_all | solution.py:247
  101.8 0.6 shard_map.63
  (4 shorter events, 0.1 us)
Async XLA Ops:
  0.6 0.8 copy-start
  1.5 0.7 copy-start.3
  12.6 15.3 %copy-start.1 = (f32[10,512]{1,0:T(8,128)S(1)}, f32[10,512]{1,0:T(8,128)}, u32[]{:S(2)}) copy-start(f32[10,512]{1,0:T(8,128)} %atoms_ref.1) | copy-start | bytes 61444
  12.6 15.3 %copy-start.2 = (f32[3,512]{1,0:T(4,128)S(1)}, f32[3,512]{1,0:T(4,128)}, u32[]{:S(2)}) copy-start(f32[3,512]{1,0:T(4,128)} %params_ref.1) | copy-start | bytes 18436
  12.6 30.9 %all-to-all-start.1 = ((f32[16,20,128]{2,1,0:T(8,128)}), f32[16,20,128]{2,1,0:T(8,128)S(1)}, u32[]{:S(2)}, u32[]{:S(2)}) async-start(f32[16,20,128]{2,1,0:T(8,128)} %shard_map.60), calls=%async_computation.1 | async-start | bytes 393216 | tf_op jit(solution)/shard_map/all_to_all | solution.py:238
  28.0 3.1 %collective-permute-start = (f32[1,16,512]{2,1,0:T(8,128)S(1)}, f32[1,16,512]{2,1,0:T(8,128)S(1)}, u32[]{:S(2)}, u32[]{:S(2)}) collective-permute-start(f32[1,16,512]{2,1,0:T(8,128)S(1)} %shard_map.61.own_ref), channel_id=1, source_target_pairs={{0,1},{1,0},{2,3},{3,2},{4,5},{5,4},{6,7},{7,6},{8,9},{9,8},{10,11... | collective-permute-start | bytes 98312 | tf_op jit(solution)/shard_map/ppermute | solution.py:227
  31.1 6.1 %collective-permute-start.1 = (f32[2,16,512]{2,1,0:T(8,128)S(1)}, f32[2,16,512]{2,1,0:T(8,128)S(1)}, u32[]{:S(2)}, u32[]{:S(2)}) collective-permute-start(f32[2,16,512]{2,1,0:T(8,128)S(1)} %pad_maximum_fusion.1), channel_id=1, source_target_pairs={{0,16},{16,0},{32,48},{48,32},{1,17},{17,1},{33,49},{49,33},{2,18}... | collective-permute-start | bytes 196616 | tf_op jit(solution)/shard_map/ppermute | solution.py:227
  37.2 12.0 %collective-permute-start.2 = (f32[4,16,512]{2,1,0:T(8,128)S(1)}, f32[4,16,512]{2,1,0:T(8,128)S(1)}, u32[]{:S(2)}, u32[]{:S(2)}) collective-permute-start(f32[4,16,512]{2,1,0:T(8,128)S(1)} %pad_maximum_fusion), channel_id=1, source_target_pairs={{0,32},{16,48},{32,0},{48,16},{1,33},{17,49},{33,1},{49,17},{2,34}... | collective-permute-start | bytes 393224 | tf_op jit(solution)/shard_map/ppermute | solution.py:227

commit v2 on v1

--- a/solution.py
+++ b/solution.py
@@ -13,6 +13,7 @@
 limit = 2.0**100
 
 ATOM_ROWS, ONE_ROW, ROWS = 10, 13, 16
+PACKED, STATES = 5, 5
 
 
 def split(values):
@@ -80,17 +81,20 @@
 
 def begin_kernel(coefs_ref, own_ref, core_ref, near_ref, plain, shifted, peak, sums, own_coefs_ref, kept, sem):
     groups = coefs_ref.shape[0] // 2
-    half = coefs_ref.shape[2]
-    mine = lax.axis_index("zl")
-    mine_sum = coefs_ref[mine] + coefs_ref[groups + mine]
-    kept[:, :half] = mine_sum[:ATOM_ROWS]
-    kept[:, half:] = mine_sum[ATOM_ROWS:]
+    half = coefs_ref.shape[3]
+
+    def rows_of(at):
+        return jnp.concatenate([coefs_ref[at, r] + coefs_ref[groups + at, r] for r in range(PACKED)], axis=0)
+
+    mine = rows_of(lax.axis_index("zl"))
+    kept[:, :half] = mine[:ATOM_ROWS]
+    kept[:, half:] = mine[ATOM_ROWS:]
     copy = pltpu.make_async_copy(kept, own_coefs_ref, sem)
     copy.start()
 
     zeros = jnp.zeros((ROWS - ATOM_ROWS, half), jnp.float32)
     for g in range(groups):
-        both = scale * (coefs_ref[g] + coefs_ref[groups + g])
+        both = scale * rows_of(g)
         for h in range(2):
             part = both[h * ATOM_ROWS : (h + 1) * ATOM_ROWS]
             at = (2 * g + h) * half
@@ -103,12 +107,12 @@
     copy.wait()
 
 
-def end_kernel(plain, shifted, first_peak, first_sums, own_ref, core_ref, near_ref, far_ref, state_ref, peak, sums):
+def end_kernel(plain, shifted, first_peak, first_sums, own_ref, core_ref, near_ref, second_ref, third_ref, state_ref, peak, sums):
     groups = state_ref.shape[0] // 2
-    width = state_ref.shape[2]
+    half = state_ref.shape[3]
     peak[...] = first_peak[...]
     sums[...] = first_sums[...]
-    add_weights((far_ref,), shifted, sums)
+    add_weights((second_ref, third_ref), shifted, sums)
     fine = jnp.all(sums[ONE_ROW : ONE_ROW + 1, :] < limit)
 
     @pl.when(jnp.logical_not(fine))
@@ -122,15 +126,18 @@
             sums[...] = sums[...] * jnp.exp2(peak[...] - top) + weigh(param_terms(piece), jnp.exp2(scores - top))
             peak[...] = top
 
-        over_pieces((own_ref, core_ref, near_ref, far_ref), step)
+        over_pieces((own_ref, core_ref, near_ref, second_ref, third_ref), step)
 
     total = sums[ONE_ROW : ONE_ROW + 1, :]
     weighted = sums[10:13, :] + sums[0:3, :] + sums[4:7, :]
+    values = (peak[...], total, weighted[0:1], weighted[1:2], weighted[2:3])
     for g in range(groups):
-        at = slice(g * width, (g + 1) * width)
-        state = jnp.concatenate([peak[:, at], total[:, at], weighted[:, at], jnp.zeros((3, width), jnp.float32)], axis=0)
-        state_ref[g] = state
-        state_ref[groups + g] = state
+        for i, value in enumerate(values):
+            for h in range(2):
+                at = (2 * g + h) * half
+                row = value[:, at : at + half]
+                state_ref[g, i, h : h + 1] = row
+                state_ref[groups + g, i, h : h + 1] = row
 
 
 def in_vmem():
@@ -138,7 +145,7 @@
 
 
 def begin(coefs, own, core, near):
-    groups, voxels = coefs.shape[0] // 2, 2 * coefs.shape[2]
+    groups, voxels = coefs.shape[0] // 2, 2 * coefs.shape[3]
     everything = groups * voxels
     return pl.pallas_call(
         begin_kernel,
@@ -161,8 +168,8 @@
     everything = plain.shape[1]
     return pl.pallas_call(
         end_kernel,
-        out_shape=shape(2 * groups, 8, everything // groups),
-        in_specs=[in_vmem()] * 8,
+        out_shape=shape(2 * groups, STATES, 2, everything // groups // 2),
+        in_specs=[in_vmem()] * 9,
         out_specs=in_vmem(),
         scratch_shapes=[pltpu.VMEM((1, everything), jnp.float32), pltpu.VMEM((ROWS, everything), jnp.float32)],
         compiler_params=pltpu.CompilerParams(vmem_limit_bytes=24 << 20),
@@ -190,9 +197,10 @@
 def project_kernel(basis_ref, signals_ref, out_ref):
     sums = jnp.dot(basis_ref[...], signals_ref[...], preferred_element_type=jnp.float32)
     half = sums.shape[1] // 2
+    rows = jnp.concatenate([sums[:, :half], sums[:, half:]], axis=0)
     for i in range(out_ref.shape[0]):
-        out_ref[i, :ATOM_ROWS] = sums[:, :half]
-        out_ref[i, ATOM_ROWS:] = sums[:, half:]
+        for r in range(PACKED):
+            out_ref[i, r] = rows[4 * r : 4 * r + 4]
 
 
 def add_kernel(parts_ref, out_ref):
@@ -202,21 +210,25 @@
 
 
 def merged(states):
-    peak = jnp.max(states[:, :1], axis=0)
-    return peak, jnp.sum(states * jnp.exp2(states[:, :1] - peak[None]), axis=0)
+    peak = jnp.max(states[:, 0], axis=0)
+    factors = jnp.exp2(states[:, 0] - peak[None])
+    return [peak] + [jnp.sum(states[:, i] * factors, axis=0) for i in range(1, STATES)]
 
 
 def merge_kernel(states_ref, out_ref):
-    peak, sums = merged(states_ref[...])
-    row = lax.broadcasted_iota(jnp.int32, sums.shape, 0)
-    state = jnp.where(row == 0, peak, sums)
+    state = merged(states_ref[...])
     for i in range(out_ref.shape[0]):
-        out_ref[i] = state
+        for j in range(STATES):
+            out_ref[i, j] = state[j]
 
 
 def finish_kernel(states_ref, maps_ref):
-    _, sums = merged(states_ref[...])
-    maps_ref[...] = sums[2:5] / sums[1:2]
+    _, total, *weighted = merged(states_ref[...])
+    half = total.shape[1]
+    for j, value in enumerate(weighted):
+        result = value / total
+        for h in range(2):
+            maps_ref[j : j + 1, h * half : (h + 1) * half] = result[h : h + 1]
 
 
 def shape(*sizes):
@@ -228,24 +240,26 @@
 
 
 def on_device(signals, basis, atoms, params):
-    width, voxels = atoms.shape[1], signals.shape[1]
+    width, half = atoms.shape[1], signals.shape[1] // 2
     across, along = lax.axis_size("x"), lax.axis_size(("zh", "zl"))
-    sums = call(project_kernel, shape(across, 2 * ATOM_ROWS, voxels // 2), basis, signals)
+    sums = call(project_kernel, shape(across, PACKED, 4, half), basis, signals)
     own = call(pack_kernel, shape(1, ROWS, width), atoms, params)
     sums = lax.all_to_all(sums, "x", 0, 0)
     core = exchange(own, "c", 1)
-    sums = call(add_kernel, shape(along, 2 * ATOM_ROWS, voxels // 2), sums)
+    sums = call(add_kernel, shape(along, PACKED, 4, half), sums)
     coefs = lax.all_to_all(sums, ("zh", "zl"), 0, 0)
-    near = exchange(jnp.concatenate([own, core]), "y", 1)
-    far = exchange(jnp.concatenate([own, core, near]), "y", 2)
+    both = jnp.concatenate([own, core])
+    near = exchange(both, "y", 1)
+    second = exchange(both, "y", 2)
+    third = exchange(both, "y", 3)
 
     groups = along // 2
     plain, shifted, peak, sums, coefficients = begin(coefs, own, core, near)
-    states = end(groups, plain, shifted, peak, sums, own, core, near, far)
+    states = end(groups, plain, shifted, peak, sums, own, core, near, second, third)
     states = lax.all_to_all(states, ("zh", "zl"), 0, 0)
-    states = call(merge_kernel, shape(across, 8, voxels), states)
+    states = call(merge_kernel, shape(across, STATES, 2, half), states)
     states = lax.all_to_all(states, "x", 0, 0)
-    maps = call(finish_kernel, shape(3, voxels), states)
+    maps = call(finish_kernel, shape(3, 2 * half), states)
     return coefficients, maps
 
 

time: 103 us -> 102 us (level)
  the two profiles are of different devices: /device:TPU:8 before, /device:TPU:24 now
where the time goes in v2:
time: 102 us; the launch traced here: 101 us
  blocking collectives  41 us (40%)
  Pallas kernels  28.2 us (28%)
  starting transfers between devices  27.7 us (27%)
  waiting for transfers between devices  2.33 us (2%)
  local copies, waits for them, and re-layouts  1.53 us (2%)
    all_to_all x1, blocking collectives, on_device(): states = lax.all_to_all(states, ('zh', 'zl'), 0, 0)  23.7 us
    pallas_call x1, Pallas kernels, end(): pl.pallas_call(end_kernel, out_shape=shape(2 * groups, STATES, 2, everyth...  21 us
    all_to_all x1, starting transfers between devices, on_device(): coefs = lax.all_to_all(sums, ('zh', 'zl'), 0, 0)  15.3 us
    ppermute x4, starting transfers between devices, exchange(): lax.ppermute(array, axis, [(i, i ^ mask) for i in range(lax.axis_size(axi...  12.3 us
    all_to_all x1, blocking collectives, on_device(): sums = lax.all_to_all(sums, 'x', 0, 0)  9.58 us
    all_to_all x1, blocking collectives, on_device(): states = lax.all_to_all(states, 'x', 0, 0)  7.73 us
    pallas_call x1, Pallas kernels, begin(): pl.pallas_call(begin_kernel, out_shape=(shape(ROWS, everything), jax.Shap...  5.68 us
  transfers between devices with their start and end apart: 5, of which 2 were waited for; matrix products, arithmetic and copies ran while one was open for 0% of the time, Pallas kernels for 6%

profile of v2, /device:TPU:24, one launch (start us, length us, event | category | flops | bytes accessed | tf_op | source)
XLA Modules:
  0.0 101.4 jit_solution(9690359717281660451)
XLA Ops:
  0.6 0.0 copy-start
  0.6 0.8 copy-done
  1.5 0.0 copy-start.3
  1.5 0.7 copy-done.3
  2.2 0.1 shard_map.59
  2.3 9.6 %all_to_all.20.parts_ref = f32[4,5,4,128]{3,2,1,0:T(4,128)S(1)} all-to-all(f32[4,5,4,128]{3,2,1,0:T(4,128)S(1)} %shard_map.59), channel_id=1, replica_groups=mesh['x'=4,'zh'=2,'y'=4,'zl'=8,'c'=2] {'x'}, dimensions={0} | all-to-all | bytes 81920 | tf_op jit(solution)/shard_map/all_to_all | solution.py:247
  11.9 0.7 shard_map.60
  12.6 0.0 copy-start.1
  12.6 0.0 copy-start.2
  12.6 15.3 %all-to-all-start.1 = ((f32[16,5,4,128]{3,2,1,0:T(4,128)}), f32[16,5,4,128]{3,2,1,0:T(4,128)S(1)}, u32[]{:S(2)}, u32[]{:S(2)}) async-start(f32[16,5,4,128]{3,2,1,0:T(4,128)} %shard_map.60), calls=%async_computation.1 | async-start | bytes 327680 | tf_op jit(solution)/shard_map/all_to_all | solution.py:250
  27.9 0.0 copy-done.1
  27.9 0.0 copy-done.2
  27.9 1.9 %collective-permute-start = (f32[1,16,512]{2,1,0:T(8,128)S(1)}, f32[1,16,512]{2,1,0:T(8,128)S(1)}, u32[]{:S(2)}, u32[]{:S(2)}) collective-permute-start(f32[1,16,512]{2,1,0:T(8,128)S(1)} %shard_map.61.own_ref), channel_id=1, source_target_pairs={{0,1},{1,0},{2,3},{3,2},{4,5},{5,4},{6,7},{7,6},{8,9},{9,8},{10,11... | collective-permute-start | bytes 98312 | tf_op jit(solution)/shard_map/ppermute | solution.py:239
  29.9 1.2 %collective-permute-done.core_ref = f32[1,16,512]{2,1,0:T(8,128)S(1)} collective-permute-done((f32[1,16,512]{2,1,0:T(8,128)S(1)}, f32[1,16,512]{2,1,0:T(8,128)S(1)}, u32[]{:S(2)}, u32[]{:S(2)}) %collective-permute-start) | collective-permute-done | bytes 32800 | tf_op jit(solution)/shard_map/ppermute | solution.py:239
  31.0 2.6 %collective-permute-start.1 = (f32[2,16,512]{2,1,0:T(8,128)S(1)}, f32[2,16,512]{2,1,0:T(8,128)S(1)}, u32[]{:S(2)}, u32[]{:S(2)}) collective-permute-start(f32[2,16,512]{2,1,0:T(8,128)S(1)} %pad_maximum_fusion), channel_id=1, source_target_pairs={{0,16},{16,0},{32,48},{48,32},{1,17},{17,1},{33,49},{49,33},{2,18}... | collective-permute-start | bytes 196616 | tf_op jit(solution)/shard_map/ppermute | solution.py:239
  33.7 2.8 %collective-permute-start.2 = (f32[2,16,512]{2,1,0:T(8,128)S(1)}, f32[2,16,512]{2,1,0:T(8,128)S(1)}, u32[]{:S(2)}, u32[]{:S(2)}) collective-permute-start(f32[2,16,512]{2,1,0:T(8,128)S(1)} %pad_maximum_fusion), channel_id=1, source_target_pairs={{0,32},{16,48},{32,0},{48,16},{1,33},{17,49},{33,1},{49,17},{2,34}... | collective-permute-start | bytes 196616 | tf_op jit(solution)/shard_map/ppermute | solution.py:239
  36.5 4.9 %collective-permute-start.3 = (f32[2,16,512]{2,1,0:T(8,128)S(1)}, f32[2,16,512]{2,1,0:T(8,128)S(1)}, u32[]{:S(2)}, u32[]{:S(2)}) collective-permute-start(f32[2,16,512]{2,1,0:T(8,128)S(1)} %pad_maximum_fusion), channel_id=1, source_target_pairs={{0,48},{16,32},{32,16},{48,0},{1,49},{17,33},{33,17},{49,1},{2,50}... | collective-permute-start | bytes 196616 | tf_op jit(solution)/shard_map/ppermute | solution.py:239
  41.5 0.0 collective-permute-done.1.near_ref
  41.5 1.1 %all-to-all-done.1.coefs_ref = f32[16,5,4,128]{3,2,1,0:T(4,128)S(1)} async-done(((f32[16,5,4,128]{3,2,1,0:T(4,128)}), f32[16,5,4,128]{3,2,1,0:T(4,128)S(1)}, u32[]{:S(2)}, u32[]{:S(2)}) %all-to-all-start.1) | async-done | bytes 163872 | tf_op jit(solution)/shard_map/all_to_all | solution.py:250
  42.6 5.7 %begin.1 = (f32[16,2048]{1,0:T(8,128)S(1)}, bf16[96,2048]{1,0:T(8,128)(2,1)S(1)}, f32[1,2048]{1,0:T(1,128)S(1)}, f32[16,2048]{1,0:T(8,128)S(1)}, f32[10,256]{1,0:T(8,128)}) custom-call(f32[16,5,4,128]{3,2,1,0:T(4,128)S(1)} %all-to-all-done.1.coefs_ref, f32[1,16,512]{2,1,0:T(8,128)S(1)} %shard_map.61.own_ref, ...), custom_call_target="tpu_custom_call" | custom-call | tf_op jit(solution)/shard_map/begin/pallas_call | solution.py:150
  48.3 0.0 collective-permute-done.2.second_ref
  48.3 0.0 collective-permute-done.3.third_ref
  48.3 21.0 %end.1 = f32[16,5,2,128]{3,2,1,0:T(2,128)S(1)} custom-call(f32[16,2048]{1,0:T(8,128)S(1)} %get-tuple-element.8.plain, bf16[96,2048]{1,0:T(8,128)(2,1)S(1)} %get-tuple-element.9.shifted, f32[1,2048]{1,0:T(1,128)S(1)} %get-tuple-element.10.first_peak, f32[16,2048]{1,0:T(8,128)S(1)} %get-tuple-element.11.first_sums, f32[1,16,512]{2,1,0:T(8,128)S(1)} %shard_map.61.own_ref, ...), custom_call_target="tpu_custom_call" | custom-call | tf_op jit(solution)/shard_map/end/pallas_call | solution.py:169
  69.4 23.7 %all_to_all.21.states_ref = f32[16,5,2,128]{3,2,1,0:T(2,128)S(1)} all-to-all(f32[16,5,2,128]{3,2,1,0:T(2,128)S(1)} %end.1), channel_id=1, replica_groups=mesh['x'=4,'zh'=2,'y'=4,'zl'=8,'c'=2] {'zh','zl'}, dimensions={0} | all-to-all | bytes 163840 | tf_op jit(solution)/shard_map/all_to_all | solution.py:259
  93.0 0.1 shard_map.62
  93.1 7.7 %all_to_all.22.states_ref = f32[4,5,2,128]{3,2,1,0:T(2,128)S(1)} all-to-all(f32[4,5,2,128]{3,2,1,0:T(2,128)S(1)} %shard_map.62), channel_id=1, replica_groups=mesh['x'=4,'zh'=2,'y'=4,'zl'=8,'c'=2] {'x'}, dimensions={0} | all-to-all | bytes 40960 | tf_op jit(solution)/shard_map/all_to_all | solution.py:261
  100.8 0.6 shard_map.63
  (2 shorter events, 0.0 us)
Async XLA Ops:
  0.6 0.8 copy-start
  1.5 0.7 copy-start.3
  12.6 15.3 %copy-start.1 = (f32[10,512]{1,0:T(8,128)S(1)}, f32[10,512]{1,0:T(8,128)}, u32[]{:S(2)}) copy-start(f32[10,512]{1,0:T(8,128)} %atoms_ref.1) | copy-start | bytes 61444
  12.6 15.3 %copy-start.2 = (f32[3,512]{1,0:T(4,128)S(1)}, f32[3,512]{1,0:T(4,128)}, u32[]{:S(2)}) copy-start(f32[3,512]{1,0:T(4,128)} %params_ref.1) | copy-start | bytes 18436
  12.6 30.1 %all-to-all-start.1 = ((f32[16,5,4,128]{3,2,1,0:T(4,128)}), f32[16,5,4,128]{3,2,1,0:T(4,128)S(1)}, u32[]{:S(2)}, u32[]{:S(2)}) async-start(f32[16,5,4,128]{3,2,1,0:T(4,128)} %shard_map.60), calls=%async_computation.1 | async-start | bytes 327680 | tf_op jit(solution)/shard_map/all_to_all | solution.py:250
  27.9 3.1 %collective-permute-start = (f32[1,16,512]{2,1,0:T(8,128)S(1)}, f32[1,16,512]{2,1,0:T(8,128)S(1)}, u32[]{:S(2)}, u32[]{:S(2)}) collective-permute-start(f32[1,16,512]{2,1,0:T(8,128)S(1)} %shard_map.61.own_ref), channel_id=1, source_target_pairs={{0,1},{1,0},{2,3},{3,2},{4,5},{5,4},{6,7},{7,6},{8,9},{9,8},{10,11... | collective-permute-start | bytes 98312 | tf_op jit(solution)/shard_map/ppermute | solution.py:239
  31.0 10.4 %collective-permute-start.1 = (f32[2,16,512]{2,1,0:T(8,128)S(1)}, f32[2,16,512]{2,1,0:T(8,128)S(1)}, u32[]{:S(2)}, u32[]{:S(2)}) collective-permute-start(f32[2,16,512]{2,1,0:T(8,128)S(1)} %pad_maximum_fusion), channel_id=1, source_target_pairs={{0,16},{16,0},{32,48},{48,32},{1,17},{17,1},{33,49},{49,33},{2,18}... | collective-permute-start | bytes 196616 | tf_op jit(solution)/shard_map/ppermute | solution.py:239
  33.7 14.6 %collective-permute-start.2 = (f32[2,16,512]{2,1,0:T(8,128)S(1)}, f32[2,16,512]{2,1,0:T(8,128)S(1)}, u32[]{:S(2)}, u32[]{:S(2)}) collective-permute-start(f32[2,16,512]{2,1,0:T(8,128)S(1)} %pad_maximum_fusion), channel_id=1, source_target_pairs={{0,32},{16,48},{32,0},{48,16},{1,33},{17,49},{33,1},{49,17},{2,34}... | collective-permute-start | bytes 196616 | tf_op jit(solution)/shard_map/ppermute | solution.py:239
  36.5 11.8 %collective-permute-start.3 = (f32[2,16,512]{2,1,0:T(8,128)S(1)}, f32[2,16,512]{2,1,0:T(8,128)S(1)}, u32[]{:S(2)}, u32[]{:S(2)}) collective-permute-start(f32[2,16,512]{2,1,0:T(8,128)S(1)} %pad_maximum_fusion), channel_id=1, source_target_pairs={{0,48},{16,32},{32,16},{48,0},{1,49},{17,33},{33,17},{49,1},{2,50}... | collective-permute-start | bytes 196616 | tf_op jit(solution)/shard_map/ppermute | solution.py:239

commit v3 on v2

--- a/solution.py
+++ b/solution.py
@@ -14,6 +14,8 @@
 
 ATOM_ROWS, ONE_ROW, ROWS = 10, 13, 16
 PACKED, STATES = 5, 5
+COEFS_FROM, STATES_FROM = 12, 8
+SAMPLE = 128
 
 
 def split(values):
@@ -79,11 +81,12 @@
     over_pieces(refs, step)
 
 
-def begin_kernel(coefs_ref, own_ref, core_ref, near_ref, plain, shifted, peak, sums, own_coefs_ref, kept, sem):
+def begin_kernel(coefs_ref, mine_ref, plain, shifted, peak, sums, own_coefs_ref, kept, sem):
     groups = coefs_ref.shape[0] // 2
     half = coefs_ref.shape[3]
 
-    def rows_of(at):
+    def rows_of(zl):
+        at = (zl + 2 * groups - COEFS_FROM) % groups
         return jnp.concatenate([coefs_ref[at, r] + coefs_ref[groups + at, r] for r in range(PACKED)], axis=0)
 
     mine = rows_of(lax.axis_index("zl"))
@@ -100,19 +103,19 @@
             at = (2 * g + h) * half
             plain[:, at : at + half] = jnp.concatenate([part, zeros], axis=0)
 
-    peak[...] = jnp.max(scores_of(atom_terms(own_ref[0]), stack(plain[...])), axis=0, keepdims=True)
+    peak[...] = jnp.max(scores_of(atom_terms(mine_ref[0])[:, :SAMPLE], stack(plain[...])), axis=0, keepdims=True)
     shifted[...] = stack(jnp.where(row_index() == ONE_ROW, -peak[...], plain[...]))
     sums[...] = jnp.zeros_like(sums)
-    add_weights((own_ref, core_ref, near_ref), shifted, sums)
+    add_weights((mine_ref,), shifted, sums)
     copy.wait()
 
 
-def end_kernel(plain, shifted, first_peak, first_sums, own_ref, core_ref, near_ref, second_ref, third_ref, state_ref, peak, sums):
+def end_kernel(plain, shifted, first_peak, first_sums, mine_ref, theirs_ref, state_ref, peak, sums):
     groups = state_ref.shape[0] // 2
     half = state_ref.shape[3]
     peak[...] = first_peak[...]
     sums[...] = first_sums[...]
-    add_weights((second_ref, third_ref), shifted, sums)
+    add_weights((theirs_ref,), shifted, sums)
     fine = jnp.all(sums[ONE_ROW : ONE_ROW + 1, :] < limit)
 
     @pl.when(jnp.logical_not(fine))
@@ -126,7 +129,7 @@
             sums[...] = sums[...] * jnp.exp2(peak[...] - top) + weigh(param_terms(piece), jnp.exp2(scores - top))
             peak[...] = top
 
-        over_pieces((own_ref, core_ref, near_ref, second_ref, third_ref), step)
+        over_pieces((mine_ref, theirs_ref), step)
 
     total = sums[ONE_ROW : ONE_ROW + 1, :]
     weighted = sums[10:13, :] + sums[0:3, :] + sums[4:7, :]
@@ -136,15 +139,16 @@
             for h in range(2):
                 at = (2 * g + h) * half
                 row = value[:, at : at + half]
-                state_ref[g, i, h : h + 1] = row
-                state_ref[groups + g, i, h : h + 1] = row
+                slot = (g - STATES_FROM) % groups
+                state_ref[slot, i, h : h + 1] = row
+                state_ref[groups + slot, i, h : h + 1] = row
 
 
 def in_vmem():
     return pl.BlockSpec(memory_space=pltpu.VMEM)
 
 
-def begin(coefs, own, core, near):
+def begin(coefs, mine):
     groups, voxels = coefs.shape[0] // 2, 2 * coefs.shape[3]
     everything = groups * voxels
     return pl.pallas_call(
@@ -156,12 +160,12 @@
             shape(ROWS, everything),
             shape(ATOM_ROWS, voxels),
         ),
-        in_specs=[in_vmem()] * 4,
+        in_specs=[in_vmem()] * 2,
         out_specs=(in_vmem(),) * 4 + (pl.BlockSpec(memory_space=pl.ANY),),
         scratch_shapes=[pltpu.VMEM((ATOM_ROWS, voxels), jnp.float32), pltpu.SemaphoreType.DMA],
         compiler_params=pltpu.CompilerParams(vmem_limit_bytes=24 << 20),
         name="begin",
-    )(coefs, own, core, near)
+    )(coefs, mine)
 
 
 def end(groups, plain, *rest):
@@ -169,7 +173,7 @@
     return pl.pallas_call(
         end_kernel,
         out_shape=shape(2 * groups, STATES, 2, everything // groups // 2),
-        in_specs=[in_vmem()] * 9,
+        in_specs=[in_vmem()] * 6,
         out_specs=in_vmem(),
         scratch_shapes=[pltpu.VMEM((1, everything), jnp.float32), pltpu.VMEM((ROWS, everything), jnp.float32)],
         compiler_params=pltpu.CompilerParams(vmem_limit_bytes=24 << 20),
@@ -181,26 +185,49 @@
     return pl.pallas_call(
         kernel,
         out_shape=shapes,
-        in_specs=[pl.BlockSpec(memory_space=pltpu.VMEM)] * len(arrays),
-        out_specs=jax.tree.map(lambda _: pl.BlockSpec(memory_space=pltpu.VMEM), shapes),
+        in_specs=[in_vmem()] * len(arrays),
+        out_specs=jax.tree.map(lambda _: in_vmem(), shapes),
         compiler_params=pltpu.CompilerParams(vmem_limit_bytes=4 << 20),
     )(*arrays)
 
 
 def pack_kernel(atoms_ref, params_ref, own_ref):
+    width = atoms_ref.shape[1]
     own_ref[0, :ATOM_ROWS] = atoms_ref[...]
     own_ref[0, ATOM_ROWS:ONE_ROW] = params_ref[...]
-    own_ref[0, ONE_ROW : ONE_ROW + 1] = jnp.ones((1, atoms_ref.shape[1]), jnp.float32)
-    own_ref[0, ONE_ROW + 1 :] = jnp.zeros((ROWS - ONE_ROW - 1, atoms_ref.shape[1]), jnp.float32)
-
-
-def project_kernel(basis_ref, signals_ref, out_ref):
-    sums = jnp.dot(basis_ref[...], signals_ref[...], preferred_element_type=jnp.float32)
+    own_ref[0, ONE_ROW : ONE_ROW + 1] = jnp.ones((1, width), jnp.float32)
+    own_ref[0, ONE_ROW + 1 :] = jnp.zeros((ROWS - ONE_ROW - 1, width), jnp.float32)
+
+
+def project_kernel(signals_ref, basis_ref, out_ref, signals, basis, sems):
+    copies = [
+        pltpu.make_async_copy(signals_ref, signals, sems.at[0]),
+        pltpu.make_async_copy(basis_ref, basis, sems.at[1]),
+    ]
+    for copy in copies:
+        copy.start()
+    for copy in copies:
+        copy.wait()
+    sums = jnp.dot(basis[...], signals[...], preferred_element_type=jnp.float32)
     half = sums.shape[1] // 2
     rows = jnp.concatenate([sums[:, :half], sums[:, half:]], axis=0)
-    for i in range(out_ref.shape[0]):
-        for r in range(PACKED):
-            out_ref[i, r] = rows[4 * r : 4 * r + 4]
+    for r in range(PACKED):
+        block = rows[4 * r : 4 * r + 4]
+        for i in range(out_ref.shape[0]):
+            out_ref[i, r] = block
+
+
+def project(signals, basis, slots):
+    arrays = [pltpu.with_memory_space_constraint(array, pltpu.HBM) for array in (signals, basis)]
+    return pl.pallas_call(
+        project_kernel,
+        out_shape=shape(slots, PACKED, 4, signals.shape[1] // 2),
+        in_specs=[pl.BlockSpec(memory_space=pltpu.HBM)] * 2,
+        out_specs=in_vmem(),
+        scratch_shapes=[pltpu.VMEM(array.shape, array.dtype) for array in arrays] + [pltpu.SemaphoreType.DMA((2,))],
+        compiler_params=pltpu.CompilerParams(vmem_limit_bytes=4 << 20),
+        name="project",
+    )(*arrays)
 
 
 def add_kernel(parts_ref, out_ref):
@@ -239,26 +266,40 @@
     return lax.ppermute(array, axis, [(i, i ^ mask) for i in range(lax.axis_size(axis))])
 
 
+def spread(array, axes):
+    order = [0]
+    for axis in axes:
+        size = lax.axis_size(axis)
+        order = [at * size + (i + size // 2) % size for at in order for i in range(size)]
+    return lax.all_to_all(array, axes, 0, 0, axis_index_groups=[order])
+
+
+def along_z(array, first):
+    count = lax.axis_size(("zh", "zl"))
+    order = [(i + first) % count for i in range(count)]
+    return lax.all_to_all(array, ("zh", "zl"), 0, 0, axis_index_groups=[order])
+
+
 def on_device(signals, basis, atoms, params):
     width, half = atoms.shape[1], signals.shape[1] // 2
     across, along = lax.axis_size("x"), lax.axis_size(("zh", "zl"))
-    sums = call(project_kernel, shape(across, PACKED, 4, half), basis, signals)
+    sums = project(signals, basis, across)
+    sums = spread(sums, ("x",))
     own = call(pack_kernel, shape(1, ROWS, width), atoms, params)
-    sums = lax.all_to_all(sums, "x", 0, 0)
-    core = exchange(own, "c", 1)
+    near = exchange(own, "y", 1)
     sums = call(add_kernel, shape(along, PACKED, 4, half), sums)
-    coefs = lax.all_to_all(sums, ("zh", "zl"), 0, 0)
-    both = jnp.concatenate([own, core])
-    near = exchange(both, "y", 1)
-    second = exchange(both, "y", 2)
-    third = exchange(both, "y", 3)
+    coefs = along_z(sums, COEFS_FROM)
+    pair = jnp.concatenate([own, near])
+    far = exchange(pair, "y", 2)
+    mine = jnp.concatenate([pair, far])
+    theirs = exchange(mine, "c", 1)
 
     groups = along // 2
-    plain, shifted, peak, sums, coefficients = begin(coefs, own, core, near)
-    states = end(groups, plain, shifted, peak, sums, own, core, near, second, third)
-    states = lax.all_to_all(states, ("zh", "zl"), 0, 0)
+    plain, shifted, peak, sums, coefficients = begin(coefs, mine)
+    states = end(groups, plain, shifted, peak, sums, mine, theirs)
+    states = along_z(states, STATES_FROM)
     states = call(merge_kernel, shape(across, STATES, 2, half), states)
-    states = lax.all_to_all(states, "x", 0, 0)
+    states = spread(states, ("x",))
     maps = call(finish_kernel, shape(3, 2 * half), states)
     return coefficients, maps
 

time: 102 us -> 93.7 us (0.919)
  the two profiles are of different devices: /device:TPU:24 before, /device:TPU:28 now
where the time goes in v3:
time: 93.7 us; the launch traced here: 93.3 us
  blocking collectives  32.5 us (35%)
  Pallas kernels  28.9 us (31%)
  starting transfers between devices  23.5 us (25%)
  waiting for transfers between devices  7.67 us (8%)
    pallas_call x1, Pallas kernels, end(): pl.pallas_call(end_kernel, out_shape=shape(2 * groups, STATES, 2, everyth...  21 us
    all_to_all x1, blocking collectives, along_z(): return lax.all_to_all(array, ('zh', 'zl'), 0, 0, axis_index_groups=[order])  16.9 us
    all_to_all x1, starting transfers between devices, along_z(): return lax.all_to_all(array, ('zh', 'zl'), 0, 0, axis_index_groups=[order])  15.8 us
    all_to_all x2, blocking collectives, spread(): return lax.all_to_all(array, axes, 0, 0, axis_index_groups=[order])  15.6 us
    ppermute x3, starting transfers between devices, exchange(): lax.ppermute(array, axis, [(i, i ^ mask) for i in range(lax.axis_size(axi...  7.7 us
    ppermute x3, waiting for transfers between devices, exchange(): lax.ppermute(array, axis, [(i, i ^ mask) for i in range(lax.axis_size(axi...  7.66 us
    pallas_call x1, Pallas kernels, begin(): pl.pallas_call(begin_kernel, out_shape=(shape(ROWS, everything), jax.Shap...  5.51 us
  transfers between devices with their start and end apart: 4, of which 2 were waited for; matrix products, arithmetic and copies ran while one was open for 0% of the time, Pallas kernels for 6%

profile of v3, /device:TPU:28, one launch (start us, length us, event | category | flops | bytes accessed | tf_op | source)
XLA Modules:
  0.0 93.3 jit_solution(1645651812031422510)
XLA Ops:
  0.6 1.0 %project.1 = f32[4,5,4,128]{3,2,1,0:T(4,128)S(1)} custom-call(bf16[125,256]{1,0:T(8,128)(2,1)} %signals_ref.1, bf16[10,125]{1,0:T(8,128)(2,1)} %basis_ref.1), custom_call_target="tpu_custom_call" | custom-call | tf_op jit(solution)/shard_map/project/pallas_call | solution.py:222
  1.6 7.8 %all_to_all.20.parts_ref = f32[4,5,4,128]{3,2,1,0:T(4,128)S(1)} all-to-all(f32[4,5,4,128]{3,2,1,0:T(4,128)S(1)} %project.1), channel_id=1, replica_groups={{256,384,0,128},{257,385,1,129},{258,386,2,130},{259,387,3,131},{260,38..., dimensions={0} | all-to-all | bytes 81920 | tf_op jit(solution)/shard_map/all_to_all | solution.py:274
  9.5 0.7 shard_map.59
  10.2 0.0 copy-start
  10.2 0.0 copy-start.1
  10.2 15.8 %all-to-all-start.1 = ((f32[16,5,4,128]{3,2,1,0:T(4,128)}), f32[16,5,4,128]{3,2,1,0:T(4,128)S(1)}, u32[]{:S(2)}, u32[]{:S(2)}) async-start(f32[16,5,4,128]{3,2,1,0:T(4,128)} %shard_map.59), calls=%async_computation.1 | async-start | bytes 327680 | tf_op jit(solution)/shard_map/all_to_all | solution.py:280
  26.0 0.0 copy-done
  26.0 0.0 copy-done.1
  26.0 2.7 %collective-permute-start = (f32[1,16,512]{2,1,0:T(8,128)S(1)}, f32[1,16,512]{2,1,0:T(8,128)S(1)}, u32[]{:S(2)}, u32[]{:S(2)}) collective-permute-start(f32[1,16,512]{2,1,0:T(8,128)S(1)} %shard_map.60), channel_id=1, source_target_pairs={{0,16},{16,0},{32,48},{48,32},{1,17},{17,1},{33,49},{49,33},{2,18}... | collective-permute-start | bytes 98312 | tf_op jit(solution)/shard_map/ppermute | solution.py:266
  28.7 3.1 %collective-permute-done = f32[1,16,512]{2,1,0:T(8,128)S(1)} collective-permute-done((f32[1,16,512]{2,1,0:T(8,128)S(1)}, f32[1,16,512]{2,1,0:T(8,128)S(1)}, u32[]{:S(2)}, u32[]{:S(2)}) %collective-permute-start) | collective-permute-done | bytes 32800 | tf_op jit(solution)/shard_map/ppermute | solution.py:266
  31.8 3.1 %collective-permute-start.1 = (f32[2,16,512]{2,1,0:T(8,128)S(1)}, f32[2,16,512]{2,1,0:T(8,128)S(1)}, u32[]{:S(2)}, u32[]{:S(2)}) collective-permute-start(f32[2,16,512]{2,1,0:T(8,128)S(1)} %pad_maximum_fusion.1), channel_id=1, source_target_pairs={{0,32},{16,48},{32,0},{48,16},{1,33},{17,49},{33,1},{49,17},{2,34}... | collective-permute-start | bytes 196616 | tf_op jit(solution)/shard_map/ppermute | solution.py:266
  35.0 4.5 %collective-permute-done.1 = f32[2,16,512]{2,1,0:T(8,128)S(1)} collective-permute-done((f32[2,16,512]{2,1,0:T(8,128)S(1)}, f32[2,16,512]{2,1,0:T(8,128)S(1)}, u32[]{:S(2)}, u32[]{:S(2)}) %collective-permute-start.1) | collective-permute-done | bytes 65568 | tf_op jit(solution)/shard_map/ppermute | solution.py:266
  39.5 1.9 %collective-permute-start.2 = (f32[4,16,512]{2,1,0:T(8,128)S(1)}, f32[4,16,512]{2,1,0:T(8,128)S(1)}, u32[]{:S(2)}, u32[]{:S(2)}) collective-permute-start(f32[4,16,512]{2,1,0:T(8,128)S(1)} %pad_maximum_fusion.mine_ref), channel_id=1, source_target_pairs={{0,1},{1,0},{2,3},{3,2},{4,5},{5,4},{6,7},{7,6},{8,9},{9,8},{10,11... | collective-permute-start | bytes 393224 | tf_op jit(solution)/shard_map/ppermute | solution.py:266
  41.4 0.0 all-to-all-done.1.coefs_ref
  41.4 5.5 %begin.1 = (f32[16,2048]{1,0:T(8,128)S(1)}, bf16[96,2048]{1,0:T(8,128)(2,1)S(1)}, f32[1,2048]{1,0:T(1,128)S(1)}, f32[16,2048]{1,0:T(8,128)S(1)}, f32[10,256]{1,0:T(8,128)}) custom-call(f32[16,5,4,128]{3,2,1,0:T(4,128)S(1)} %all-to-all-done.1.coefs_ref, f32[4,16,512]{2,1,0:T(8,128)S(1)} %pad_maximum_fusion.mine_ref), custom_call_target="tpu_custom_call" | custom-call | tf_op jit(solution)/shard_map/begin/pallas_call | solution.py:154
  46.9 0.0 collective-permute-done.2.theirs_ref
  46.9 21.0 %end.1 = f32[16,5,2,128]{3,2,1,0:T(2,128)S(1)} custom-call(f32[16,2048]{1,0:T(8,128)S(1)} %get-tuple-element.8.plain, bf16[96,2048]{1,0:T(8,128)(2,1)S(1)} %get-tuple-element.9.shifted, f32[1,2048]{1,0:T(1,128)S(1)} %get-tuple-element.10.first_peak, f32[16,2048]{1,0:T(8,128)S(1)} %get-tuple-element.11.first_sums, ...), custom_call_target="tpu_custom_call" | custom-call | tf_op jit(solution)/shard_map/end/pallas_call | solution.py:173
  68.0 16.9 %all_to_all.21.states_ref = f32[16,5,2,128]{3,2,1,0:T(2,128)S(1)} all-to-all(f32[16,5,2,128]{3,2,1,0:T(2,128)S(1)} %end.1), channel_id=1, replica_groups={{64,66,68,70,72,74,76,78,0,2,4,6,8,10,12,14},{65,67,69,71,73,75,77,79,1..., dimensions={0} | all-to-all | bytes 163840 | tf_op jit(solution)/shard_map/all_to_all | solution.py:280
  84.9 0.1 shard_map.61
  84.9 7.7 %all_to_all.22.states_ref = f32[4,5,2,128]{3,2,1,0:T(2,128)S(1)} all-to-all(f32[4,5,2,128]{3,2,1,0:T(2,128)S(1)} %shard_map.61), channel_id=1, replica_groups={{256,384,0,128},{257,385,1,129},{258,386,2,130},{259,387,3,131},{260,38..., dimensions={0} | all-to-all | bytes 40960 | tf_op jit(solution)/shard_map/all_to_all | solution.py:274
  92.7 0.6 shard_map.62
  (3 shorter events, 0.0 us)
Async XLA Ops:
  10.2 15.8 %copy-start = (f32[10,512]{1,0:T(8,128)S(1)}, f32[10,512]{1,0:T(8,128)}, u32[]{:S(2)}) copy-start(f32[10,512]{1,0:T(8,128)} %atoms_ref.1) | copy-start | bytes 61444
  10.2 15.8 %copy-start.1 = (f32[3,512]{1,0:T(4,128)S(1)}, f32[3,512]{1,0:T(4,128)}, u32[]{:S(2)}) copy-start(f32[3,512]{1,0:T(4,128)} %params_ref.1) | copy-start | bytes 18436
  10.2 31.2 %all-to-all-start.1 = ((f32[16,5,4,128]{3,2,1,0:T(4,128)}), f32[16,5,4,128]{3,2,1,0:T(4,128)S(1)}, u32[]{:S(2)}, u32[]{:S(2)}) async-start(f32[16,5,4,128]{3,2,1,0:T(4,128)} %shard_map.59), calls=%async_computation.1 | async-start | bytes 327680 | tf_op jit(solution)/shard_map/all_to_all | solution.py:280
  26.0 5.8 %collective-permute-start = (f32[1,16,512]{2,1,0:T(8,128)S(1)}, f32[1,16,512]{2,1,0:T(8,128)S(1)}, u32[]{:S(2)}, u32[]{:S(2)}) collective-permute-start(f32[1,16,512]{2,1,0:T(8,128)S(1)} %shard_map.60), channel_id=1, source_target_pairs={{0,16},{16,0},{32,48},{48,32},{1,17},{17,1},{33,49},{49,33},{2,18}... | collective-permute-start | bytes 98312 | tf_op jit(solution)/shard_map/ppermute | solution.py:266
  31.8 7.7 %collective-permute-start.1 = (f32[2,16,512]{2,1,0:T(8,128)S(1)}, f32[2,16,512]{2,1,0:T(8,128)S(1)}, u32[]{:S(2)}, u32[]{:S(2)}) collective-permute-start(f32[2,16,512]{2,1,0:T(8,128)S(1)} %pad_maximum_fusion.1), channel_id=1, source_target_pairs={{0,32},{16,48},{32,0},{48,16},{1,33},{17,49},{33,1},{49,17},{2,34}... | collective-permute-start | bytes 196616 | tf_op jit(solution)/shard_map/ppermute | solution.py:266
  39.5 7.5 %collective-permute-start.2 = (f32[4,16,512]{2,1,0:T(8,128)S(1)}, f32[4,16,512]{2,1,0:T(8,128)S(1)}, u32[]{:S(2)}, u32[]{:S(2)}) collective-permute-start(f32[4,16,512]{2,1,0:T(8,128)S(1)} %pad_maximum_fusion.mine_ref), channel_id=1, source_target_pairs={{0,1},{1,0},{2,3},{3,2},{4,5},{5,4},{6,7},{7,6},{8,9},{9,8},{10,11... | collective-permute-start | bytes 393224 | tf_op jit(solution)/shard_map/ppermute | solution.py:266

commit v4 on v3

--- a/solution.py
+++ b/solution.py
@@ -10,11 +10,11 @@
 
 
 scale = 1.5 * math.log2(math.e)
-limit = 2.0**100
+margin, limit = 80.0, 2.0**120
 
 ATOM_ROWS, ONE_ROW, ROWS = 10, 13, 16
 PACKED, STATES = 5, 5
-COEFS_FROM, STATES_FROM = 12, 8
+COEFS_FROM, STATES_FROM = 10, 8
 SAMPLE = 128
 
 
@@ -81,7 +81,7 @@
     over_pieces(refs, step)
 
 
-def begin_kernel(coefs_ref, mine_ref, plain, shifted, peak, sums, own_coefs_ref, kept, sem):
+def begin_kernel(coefs_ref, near_ref, plain, shifted, peak, sums, own_coefs_ref, kept, sem):
     groups = coefs_ref.shape[0] // 2
     half = coefs_ref.shape[3]
 
@@ -103,19 +103,20 @@
             at = (2 * g + h) * half
             plain[:, at : at + half] = jnp.concatenate([part, zeros], axis=0)
 
-    peak[...] = jnp.max(scores_of(atom_terms(mine_ref[0])[:, :SAMPLE], stack(plain[...])), axis=0, keepdims=True)
+    sample = scores_of(atom_terms(near_ref[0])[:, :SAMPLE], stack(plain[...]))
+    peak[...] = margin + jnp.max(sample, axis=0, keepdims=True)
     shifted[...] = stack(jnp.where(row_index() == ONE_ROW, -peak[...], plain[...]))
     sums[...] = jnp.zeros_like(sums)
-    add_weights((mine_ref,), shifted, sums)
+    add_weights((near_ref,), shifted, sums)
     copy.wait()
 
 
-def end_kernel(plain, shifted, first_peak, first_sums, mine_ref, theirs_ref, state_ref, peak, sums):
+def end_kernel(plain, shifted, first_peak, first_sums, near_ref, far_ref, state_ref, peak, sums):
     groups = state_ref.shape[0] // 2
     half = state_ref.shape[3]
     peak[...] = first_peak[...]
     sums[...] = first_sums[...]
-    add_weights((theirs_ref,), shifted, sums)
+    add_weights((far_ref,), shifted, sums)
     fine = jnp.all(sums[ONE_ROW : ONE_ROW + 1, :] < limit)
 
     @pl.when(jnp.logical_not(fine))
@@ -129,11 +130,13 @@
             sums[...] = sums[...] * jnp.exp2(peak[...] - top) + weigh(param_terms(piece), jnp.exp2(scores - top))
             peak[...] = top
 
-        over_pieces((mine_ref, theirs_ref), step)
+        over_pieces((near_ref, far_ref), step)
 
     total = sums[ONE_ROW : ONE_ROW + 1, :]
-    weighted = sums[10:13, :] + sums[0:3, :] + sums[4:7, :]
-    values = (peak[...], total, weighted[0:1], weighted[1:2], weighted[2:3])
+    shift = jnp.round(jnp.log2(total))
+    down = jnp.exp2(-shift)
+    weighted = (sums[10:13, :] + sums[0:3, :] + sums[4:7, :]) * down
+    values = (peak[...] + shift, total * down, weighted[0:1], weighted[1:2], weighted[2:3])
     for g in range(groups):
         for i, value in enumerate(values):
             for h in range(2):
@@ -290,13 +293,13 @@
     sums = call(add_kernel, shape(along, PACKED, 4, half), sums)
     coefs = along_z(sums, COEFS_FROM)
     pair = jnp.concatenate([own, near])
-    far = exchange(pair, "y", 2)
-    mine = jnp.concatenate([pair, far])
-    theirs = exchange(mine, "c", 1)
+    core = exchange(pair, "c", 1)
+    four = jnp.concatenate([pair, core])
+    far = exchange(four, "y", 2)
 
     groups = along // 2
-    plain, shifted, peak, sums, coefficients = begin(coefs, mine)
-    states = end(groups, plain, shifted, peak, sums, mine, theirs)
+    plain, shifted, peak, sums, coefficients = begin(coefs, four)
+    states = end(groups, plain, shifted, peak, sums, four, far)
     states = along_z(states, STATES_FROM)
     states = call(merge_kernel, shape(across, STATES, 2, half), states)
     states = spread(states, ("x",))

time: 93.7 us -> 93.2 us (level)
  the two profiles are of different devices: /device:TPU:28 before, /device:TPU:4 now
where the time goes in v4:
time: 93.2 us; the launch traced here: 92.7 us
  blocking collectives  36.4 us (39%)
  Pallas kernels  28.9 us (31%)
  starting transfers between devices  23.1 us (25%)
  waiting for transfers between devices  3.54 us (4%)
    pallas_call x1, Pallas kernels, end(): pl.pallas_call(end_kernel, out_shape=shape(2 * groups, STATES, 2, everyth...  21 us
    all_to_all x2, blocking collectives, spread(): return lax.all_to_all(array, axes, 0, 0, axis_index_groups=[order])  20.1 us
    all_to_all x1, blocking collectives, along_z(): return lax.all_to_all(array, ('zh', 'zl'), 0, 0, axis_index_groups=[order])  16.3 us
    all_to_all x1, starting transfers between devices, along_z(): return lax.all_to_all(array, ('zh', 'zl'), 0, 0, axis_index_groups=[order])  12.6 us
    ppermute x3, starting transfers between devices, exchange(): lax.ppermute(array, axis, [(i, i ^ mask) for i in range(lax.axis_size(axi...  10.5 us
    pallas_call x1, Pallas kernels, begin(): pl.pallas_call(begin_kernel, out_shape=(shape(ROWS, everything), jax.Shap...  5.52 us
    ppermute x3, waiting for transfers between devices, exchange(): lax.ppermute(array, axis, [(i, i ^ mask) for i in range(lax.axis_size(axi...  3.54 us
  transfers between devices with their start and end apart: 4, of which 2 were waited for; matrix products, arithmetic and copies ran while one was open for 0% of the time, Pallas kernels for 6%

profile of v4, /device:TPU:4, one launch (start us, length us, event | category | flops | bytes accessed | tf_op | source)
XLA Modules:
  0.0 92.7 jit_solution(6659002001011878957)
XLA Ops:
  0.6 1.0 %project.1 = f32[4,5,4,128]{3,2,1,0:T(4,128)S(1)} custom-call(bf16[125,256]{1,0:T(8,128)(2,1)} %signals_ref.1, bf16[10,125]{1,0:T(8,128)(2,1)} %basis_ref.1), custom_call_target="tpu_custom_call" | custom-call | tf_op jit(solution)/shard_map/project/pallas_call | solution.py:225
  1.6 12.4 %all_to_all.20.parts_ref = f32[4,5,4,128]{3,2,1,0:T(4,128)S(1)} all-to-all(f32[4,5,4,128]{3,2,1,0:T(4,128)S(1)} %project.1), channel_id=1, replica_groups={{256,384,0,128},{257,385,1,129},{258,386,2,130},{259,387,3,131},{260,38..., dimensions={0} | all-to-all | bytes 81920 | tf_op jit(solution)/shard_map/all_to_all | solution.py:277
  14.0 0.7 shard_map.59
  14.7 0.0 copy-start
  14.7 0.0 copy-start.1
  14.7 12.6 %all-to-all-start.1 = ((f32[16,5,4,128]{3,2,1,0:T(4,128)}), f32[16,5,4,128]{3,2,1,0:T(4,128)S(1)}, u32[]{:S(2)}, u32[]{:S(2)}) async-start(f32[16,5,4,128]{3,2,1,0:T(4,128)} %shard_map.59), calls=%async_computation.1 | async-start | bytes 327680 | tf_op jit(solution)/shard_map/all_to_all | solution.py:283
  27.4 0.0 copy-done
  27.4 0.0 copy-done.1
  27.4 3.5 %collective-permute-start = (f32[1,16,512]{2,1,0:T(8,128)S(1)}, f32[1,16,512]{2,1,0:T(8,128)S(1)}, u32[]{:S(2)}, u32[]{:S(2)}) collective-permute-start(f32[1,16,512]{2,1,0:T(8,128)S(1)} %shard_map.60), channel_id=1, source_target_pairs={{0,16},{16,0},{32,48},{48,32},{1,17},{17,1},{33,49},{49,33},{2,18}... | collective-permute-start | bytes 98312 | tf_op jit(solution)/shard_map/ppermute | solution.py:269
  30.9 2.3 %collective-permute-done = f32[1,16,512]{2,1,0:T(8,128)S(1)} collective-permute-done((f32[1,16,512]{2,1,0:T(8,128)S(1)}, f32[1,16,512]{2,1,0:T(8,128)S(1)}, u32[]{:S(2)}, u32[]{:S(2)}) %collective-permute-start) | collective-permute-done | bytes 32800 | tf_op jit(solution)/shard_map/ppermute | solution.py:269
  33.2 1.9 %collective-permute-start.1 = (f32[2,16,512]{2,1,0:T(8,128)S(1)}, f32[2,16,512]{2,1,0:T(8,128)S(1)}, u32[]{:S(2)}, u32[]{:S(2)}) collective-permute-start(f32[2,16,512]{2,1,0:T(8,128)S(1)} %pad_maximum_fusion.1), channel_id=1, source_target_pairs={{0,1},{1,0},{2,3},{3,2},{4,5},{5,4},{6,7},{7,6},{8,9},{9,8},{10,11... | collective-permute-start | bytes 196616 | tf_op jit(solution)/shard_map/ppermute | solution.py:269
  35.1 1.2 %collective-permute-done.1 = f32[2,16,512]{2,1,0:T(8,128)S(1)} collective-permute-done((f32[2,16,512]{2,1,0:T(8,128)S(1)}, f32[2,16,512]{2,1,0:T(8,128)S(1)}, u32[]{:S(2)}, u32[]{:S(2)}) %collective-permute-start.1) | collective-permute-done | bytes 65568 | tf_op jit(solution)/shard_map/ppermute | solution.py:269
  36.3 5.1 %collective-permute-start.2 = (f32[4,16,512]{2,1,0:T(8,128)S(1)}, f32[4,16,512]{2,1,0:T(8,128)S(1)}, u32[]{:S(2)}, u32[]{:S(2)}) collective-permute-start(f32[4,16,512]{2,1,0:T(8,128)S(1)} %pad_maximum_fusion.near_ref), channel_id=1, source_target_pairs={{0,32},{16,48},{32,0},{48,16},{1,33},{17,49},{33,1},{49,17},{2,34}... | collective-permute-start | bytes 393224 | tf_op jit(solution)/shard_map/ppermute | solution.py:269
  41.5 0.0 all-to-all-done.1.coefs_ref
  41.5 5.5 %begin.1 = (f32[16,2048]{1,0:T(8,128)S(1)}, bf16[96,2048]{1,0:T(8,128)(2,1)S(1)}, f32[1,2048]{1,0:T(1,128)S(1)}, f32[16,2048]{1,0:T(8,128)S(1)}, f32[10,256]{1,0:T(8,128)}) custom-call(f32[16,5,4,128]{3,2,1,0:T(4,128)S(1)} %all-to-all-done.1.coefs_ref, f32[4,16,512]{2,1,0:T(8,128)S(1)} %pad_maximum_fusion.near_ref), custom_call_target="tpu_custom_call" | custom-call | tf_op jit(solution)/shard_map/begin/pallas_call | solution.py:157
  47.0 0.0 collective-permute-done.2.far_ref
  47.0 21.0 %end.1 = f32[16,5,2,128]{3,2,1,0:T(2,128)S(1)} custom-call(f32[16,2048]{1,0:T(8,128)S(1)} %get-tuple-element.8.plain, bf16[96,2048]{1,0:T(8,128)(2,1)S(1)} %get-tuple-element.9.shifted, f32[1,2048]{1,0:T(1,128)S(1)} %get-tuple-element.10.first_peak, f32[16,2048]{1,0:T(8,128)S(1)} %get-tuple-element.11.first_sums, ...), custom_call_target="tpu_custom_call" | custom-call | tf_op jit(solution)/shard_map/end/pallas_call | solution.py:176
  68.0 16.3 %all_to_all.21.states_ref = f32[16,5,2,128]{3,2,1,0:T(2,128)S(1)} all-to-all(f32[16,5,2,128]{3,2,1,0:T(2,128)S(1)} %end.1), channel_id=1, replica_groups={{64,66,68,70,72,74,76,78,0,2,4,6,8,10,12,14},{65,67,69,71,73,75,77,79,1..., dimensions={0} | all-to-all | bytes 163840 | tf_op jit(solution)/shard_map/all_to_all | solution.py:283
  84.3 0.1 shard_map.61
  84.4 7.7 %all_to_all.22.states_ref = f32[4,5,2,128]{3,2,1,0:T(2,128)S(1)} all-to-all(f32[4,5,2,128]{3,2,1,0:T(2,128)S(1)} %shard_map.61), channel_id=1, replica_groups={{256,384,0,128},{257,385,1,129},{258,386,2,130},{259,387,3,131},{260,38..., dimensions={0} | all-to-all | bytes 40960 | tf_op jit(solution)/shard_map/all_to_all | solution.py:277
  92.1 0.6 shard_map.62
  (3 shorter events, 0.0 us)
Async XLA Ops:
  14.7 12.6 %copy-start = (f32[10,512]{1,0:T(8,128)S(1)}, f32[10,512]{1,0:T(8,128)}, u32[]{:S(2)}) copy-start(f32[10,512]{1,0:T(8,128)} %atoms_ref.1) | copy-start | bytes 61444
  14.7 12.6 %copy-start.1 = (f32[3,512]{1,0:T(4,128)S(1)}, f32[3,512]{1,0:T(4,128)}, u32[]{:S(2)}) copy-start(f32[3,512]{1,0:T(4,128)} %params_ref.1) | copy-start | bytes 18436
  14.7 26.7 %all-to-all-start.1 = ((f32[16,5,4,128]{3,2,1,0:T(4,128)}), f32[16,5,4,128]{3,2,1,0:T(4,128)S(1)}, u32[]{:S(2)}, u32[]{:S(2)}) async-start(f32[16,5,4,128]{3,2,1,0:T(4,128)} %shard_map.59), calls=%async_computation.1 | async-start | bytes 327680 | tf_op jit(solution)/shard_map/all_to_all | solution.py:283
  27.4 5.8 %collective-permute-start = (f32[1,16,512]{2,1,0:T(8,128)S(1)}, f32[1,16,512]{2,1,0:T(8,128)S(1)}, u32[]{:S(2)}, u32[]{:S(2)}) collective-permute-start(f32[1,16,512]{2,1,0:T(8,128)S(1)} %shard_map.60), channel_id=1, source_target_pairs={{0,16},{16,0},{32,48},{48,32},{1,17},{17,1},{33,49},{49,33},{2,18}... | collective-permute-start | bytes 98312 | tf_op jit(solution)/shard_map/ppermute | solution.py:269
  33.2 3.1 %collective-permute-start.1 = (f32[2,16,512]{2,1,0:T(8,128)S(1)}, f32[2,16,512]{2,1,0:T(8,128)S(1)}, u32[]{:S(2)}, u32[]{:S(2)}) collective-permute-start(f32[2,16,512]{2,1,0:T(8,128)S(1)} %pad_maximum_fusion.1), channel_id=1, source_target_pairs={{0,1},{1,0},{2,3},{3,2},{4,5},{5,4},{6,7},{7,6},{8,9},{9,8},{10,11... | collective-permute-start | bytes 196616 | tf_op jit(solution)/shard_map/ppermute | solution.py:269
  36.3 10.6 %collective-permute-start.2 = (f32[4,16,512]{2,1,0:T(8,128)S(1)}, f32[4,16,512]{2,1,0:T(8,128)S(1)}, u32[]{:S(2)}, u32[]{:S(2)}) collective-permute-start(f32[4,16,512]{2,1,0:T(8,128)S(1)} %pad_maximum_fusion.near_ref), channel_id=1, source_target_pairs={{0,32},{16,48},{32,0},{48,16},{1,33},{17,49},{33,1},{49,17},{2,34}... | collective-permute-start | bytes 393224 | tf_op jit(solution)/shard_map/ppermute | solution.py:269

commit v5 on v4

--- a/solution.py
+++ b/solution.py
@@ -16,6 +16,7 @@
 PACKED, STATES = 5, 5
 COEFS_FROM, STATES_FROM = 10, 8
 SAMPLE = 128
+TILE = 1024
 
 
 def split(values):
@@ -73,12 +74,14 @@
             lax.fori_loop(0, count, lambda i, _, pieces=pieces: (step(pieces, i), 0)[1], 0)
 
 
-def add_weights(refs, shifted, sums):
-    def step(pieces, i):
+def add_weights(pieces, shifted, sums):
+    everything = shifted.shape[1]
+    for i in range(pieces.shape[0]):
         piece = pieces[i]
-        sums[...] += weigh(param_terms(piece), jnp.exp2(scores_of(atom_terms(piece), shifted[...])))
-
-    over_pieces(refs, step)
+        atoms, params = atom_terms(piece), param_terms(piece)
+        for at in range(0, everything, TILE):
+            tile = slice(at, at + TILE)
+            sums[:, tile] += weigh(params, jnp.exp2(scores_of(atoms, shifted[:, tile])))
 
 
 def begin_kernel(coefs_ref, near_ref, plain, shifted, peak, sums, own_coefs_ref, kept, sem):
@@ -107,7 +110,7 @@
     peak[...] = margin + jnp.max(sample, axis=0, keepdims=True)
     shifted[...] = stack(jnp.where(row_index() == ONE_ROW, -peak[...], plain[...]))
     sums[...] = jnp.zeros_like(sums)
-    add_weights((near_ref,), shifted, sums)
+    add_weights(near_ref, shifted, sums)
     copy.wait()
 
 
@@ -116,7 +119,7 @@
     half = state_ref.shape[3]
     peak[...] = first_peak[...]
     sums[...] = first_sums[...]
-    add_weights((far_ref,), shifted, sums)
+    add_weights(far_ref, shifted, sums)
     fine = jnp.all(sums[ONE_ROW : ONE_ROW + 1, :] < limit)
 
     @pl.when(jnp.logical_not(fine))

time: 93.2 us -> 92.8 us (level)
  no operation moved by 1% of the time
where the time goes in v5:
time: 92.8 us; the launch traced here: 92.3 us
  blocking collectives  36.4 us (39%)
  Pallas kernels  28.5 us (31%)
  starting transfers between devices  23.1 us (25%)
  waiting for transfers between devices  3.54 us (4%)
    pallas_call x1, Pallas kernels, end(): pl.pallas_call(end_kernel, out_shape=shape(2 * groups, STATES, 2, everyth...  20.7 us
    all_to_all x2, blocking collectives, spread(): return lax.all_to_all(array, axes, 0, 0, axis_index_groups=[order])  20.1 us
    all_to_all x1, blocking collectives, along_z(): return lax.all_to_all(array, ('zh', 'zl'), 0, 0, axis_index_groups=[order])  16.3 us
    all_to_all x1, starting transfers between devices, along_z(): return lax.all_to_all(array, ('zh', 'zl'), 0, 0, axis_index_groups=[order])  12.6 us
    ppermute x3, starting transfers between devices, exchange(): lax.ppermute(array, axis, [(i, i ^ mask) for i in range(lax.axis_size(axi...  10.5 us
    pallas_call x1, Pallas kernels, begin(): pl.pallas_call(begin_kernel, out_shape=(shape(ROWS, everything), jax.Shap...  5.44 us
    ppermute x3, waiting for transfers between devices, exchange(): lax.ppermute(array, axis, [(i, i ^ mask) for i in range(lax.axis_size(axi...  3.54 us
  transfers between devices with their start and end apart: 4, of which 2 were waited for; matrix products, arithmetic and copies ran while one was open for 0% of the time, Pallas kernels for 6%

profile of v5, /device:TPU:4, one launch (start us, length us, event | category | flops | bytes accessed | tf_op | source)
XLA Modules:
  0.0 92.3 jit_solution(5009903068447935579)
XLA Ops:
  0.6 1.0 %project.1 = f32[4,5,4,128]{3,2,1,0:T(4,128)S(1)} custom-call(bf16[125,256]{1,0:T(8,128)(2,1)} %signals_ref.1, bf16[10,125]{1,0:T(8,128)(2,1)} %basis_ref.1), custom_call_target="tpu_custom_call" | custom-call | tf_op jit(solution)/shard_map/project/pallas_call | solution.py:228
  1.6 12.4 %all_to_all.20.parts_ref = f32[4,5,4,128]{3,2,1,0:T(4,128)S(1)} all-to-all(f32[4,5,4,128]{3,2,1,0:T(4,128)S(1)} %project.1), channel_id=1, replica_groups={{256,384,0,128},{257,385,1,129},{258,386,2,130},{259,387,3,131},{260,38..., dimensions={0} | all-to-all | bytes 81920 | tf_op jit(solution)/shard_map/all_to_all | solution.py:280
  14.0 0.7 shard_map.59
  14.7 0.0 copy-start
  14.7 0.0 copy-start.1
  14.7 12.6 %all-to-all-start.1 = ((f32[16,5,4,128]{3,2,1,0:T(4,128)}), f32[16,5,4,128]{3,2,1,0:T(4,128)S(1)}, u32[]{:S(2)}, u32[]{:S(2)}) async-start(f32[16,5,4,128]{3,2,1,0:T(4,128)} %shard_map.59), calls=%async_computation.1 | async-start | bytes 327680 | tf_op jit(solution)/shard_map/all_to_all | solution.py:286
  27.4 0.0 copy-done
  27.4 0.0 copy-done.1
  27.4 3.5 %collective-permute-start = (f32[1,16,512]{2,1,0:T(8,128)S(1)}, f32[1,16,512]{2,1,0:T(8,128)S(1)}, u32[]{:S(2)}, u32[]{:S(2)}) collective-permute-start(f32[1,16,512]{2,1,0:T(8,128)S(1)} %shard_map.60), channel_id=1, source_target_pairs={{0,16},{16,0},{32,48},{48,32},{1,17},{17,1},{33,49},{49,33},{2,18}... | collective-permute-start | bytes 98312 | tf_op jit(solution)/shard_map/ppermute | solution.py:272
  30.9 2.3 %collective-permute-done = f32[1,16,512]{2,1,0:T(8,128)S(1)} collective-permute-done((f32[1,16,512]{2,1,0:T(8,128)S(1)}, f32[1,16,512]{2,1,0:T(8,128)S(1)}, u32[]{:S(2)}, u32[]{:S(2)}) %collective-permute-start) | collective-permute-done | bytes 32800 | tf_op jit(solution)/shard_map/ppermute | solution.py:272
  33.2 1.9 %collective-permute-start.1 = (f32[2,16,512]{2,1,0:T(8,128)S(1)}, f32[2,16,512]{2,1,0:T(8,128)S(1)}, u32[]{:S(2)}, u32[]{:S(2)}) collective-permute-start(f32[2,16,512]{2,1,0:T(8,128)S(1)} %pad_maximum_fusion.1), channel_id=1, source_target_pairs={{0,1},{1,0},{2,3},{3,2},{4,5},{5,4},{6,7},{7,6},{8,9},{9,8},{10,11... | collective-permute-start | bytes 196616 | tf_op jit(solution)/shard_map/ppermute | solution.py:272
  35.1 1.2 %collective-permute-done.1 = f32[2,16,512]{2,1,0:T(8,128)S(1)} collective-permute-done((f32[2,16,512]{2,1,0:T(8,128)S(1)}, f32[2,16,512]{2,1,0:T(8,128)S(1)}, u32[]{:S(2)}, u32[]{:S(2)}) %collective-permute-start.1) | collective-permute-done | bytes 65568 | tf_op jit(solution)/shard_map/ppermute | solution.py:272
  36.3 5.1 %collective-permute-start.2 = (f32[4,16,512]{2,1,0:T(8,128)S(1)}, f32[4,16,512]{2,1,0:T(8,128)S(1)}, u32[]{:S(2)}, u32[]{:S(2)}) collective-permute-start(f32[4,16,512]{2,1,0:T(8,128)S(1)} %pad_maximum_fusion.near_ref), channel_id=1, source_target_pairs={{0,32},{16,48},{32,0},{48,16},{1,33},{17,49},{33,1},{49,17},{2,34}... | collective-permute-start | bytes 393224 | tf_op jit(solution)/shard_map/ppermute | solution.py:272
  41.5 0.0 all-to-all-done.1.coefs_ref
  41.5 5.4 %begin.1 = (f32[16,2048]{1,0:T(8,128)S(1)}, bf16[96,2048]{1,0:T(8,128)(2,1)S(1)}, f32[1,2048]{1,0:T(1,128)S(1)}, f32[16,2048]{1,0:T(8,128)S(1)}, f32[10,256]{1,0:T(8,128)}) custom-call(f32[16,5,4,128]{3,2,1,0:T(4,128)S(1)} %all-to-all-done.1.coefs_ref, f32[4,16,512]{2,1,0:T(8,128)S(1)} %pad_maximum_fusion.near_ref), custom_call_target="tpu_custom_call" | custom-call | tf_op jit(solution)/shard_map/begin/pallas_call | solution.py:160
  46.9 0.0 collective-permute-done.2.far_ref
  46.9 20.7 %end.1 = f32[16,5,2,128]{3,2,1,0:T(2,128)S(1)} custom-call(f32[16,2048]{1,0:T(8,128)S(1)} %get-tuple-element.8.plain, bf16[96,2048]{1,0:T(8,128)(2,1)S(1)} %get-tuple-element.9.shifted, f32[1,2048]{1,0:T(1,128)S(1)} %get-tuple-element.10.first_peak, f32[16,2048]{1,0:T(8,128)S(1)} %get-tuple-element.11.first_sums, ...), custom_call_target="tpu_custom_call" | custom-call | tf_op jit(solution)/shard_map/end/pallas_call | solution.py:179
  67.7 16.3 %all_to_all.21.states_ref = f32[16,5,2,128]{3,2,1,0:T(2,128)S(1)} all-to-all(f32[16,5,2,128]{3,2,1,0:T(2,128)S(1)} %end.1), channel_id=1, replica_groups={{64,66,68,70,72,74,76,78,0,2,4,6,8,10,12,14},{65,67,69,71,73,75,77,79,1..., dimensions={0} | all-to-all | bytes 163840 | tf_op jit(solution)/shard_map/all_to_all | solution.py:286
  83.9 0.1 shard_map.61
  84.0 7.7 %all_to_all.22.states_ref = f32[4,5,2,128]{3,2,1,0:T(2,128)S(1)} all-to-all(f32[4,5,2,128]{3,2,1,0:T(2,128)S(1)} %shard_map.61), channel_id=1, replica_groups={{256,384,0,128},{257,385,1,129},{258,386,2,130},{259,387,3,131},{260,38..., dimensions={0} | all-to-all | bytes 40960 | tf_op jit(solution)/shard_map/all_to_all | solution.py:280
  91.7 0.6 shard_map.62
  (3 shorter events, 0.0 us)
Async XLA Ops:
  14.7 12.6 %copy-start = (f32[10,512]{1,0:T(8,128)S(1)}, f32[10,512]{1,0:T(8,128)}, u32[]{:S(2)}) copy-start(f32[10,512]{1,0:T(8,128)} %atoms_ref.1) | copy-start | bytes 61444
  14.7 12.6 %copy-start.1 = (f32[3,512]{1,0:T(4,128)S(1)}, f32[3,512]{1,0:T(4,128)}, u32[]{:S(2)}) copy-start(f32[3,512]{1,0:T(4,128)} %params_ref.1) | copy-start | bytes 18436
  14.7 26.7 %all-to-all-start.1 = ((f32[16,5,4,128]{3,2,1,0:T(4,128)}), f32[16,5,4,128]{3,2,1,0:T(4,128)S(1)}, u32[]{:S(2)}, u32[]{:S(2)}) async-start(f32[16,5,4,128]{3,2,1,0:T(4,128)} %shard_map.59), calls=%async_computation.1 | async-start | bytes 327680 | tf_op jit(solution)/shard_map/all_to_all | solution.py:286
  27.4 5.8 %collective-permute-start = (f32[1,16,512]{2,1,0:T(8,128)S(1)}, f32[1,16,512]{2,1,0:T(8,128)S(1)}, u32[]{:S(2)}, u32[]{:S(2)}) collective-permute-start(f32[1,16,512]{2,1,0:T(8,128)S(1)} %shard_map.60), channel_id=1, source_target_pairs={{0,16},{16,0},{32,48},{48,32},{1,17},{17,1},{33,49},{49,33},{2,18}... | collective-permute-start | bytes 98312 | tf_op jit(solution)/shard_map/ppermute | solution.py:272
  33.2 3.1 %collective-permute-start.1 = (f32[2,16,512]{2,1,0:T(8,128)S(1)}, f32[2,16,512]{2,1,0:T(8,128)S(1)}, u32[]{:S(2)}, u32[]{:S(2)}) collective-permute-start(f32[2,16,512]{2,1,0:T(8,128)S(1)} %pad_maximum_fusion.1), channel_id=1, source_target_pairs={{0,1},{1,0},{2,3},{3,2},{4,5},{5,4},{6,7},{7,6},{8,9},{9,8},{10,11... | collective-permute-start | bytes 196616 | tf_op jit(solution)/shard_map/ppermute | solution.py:272
  36.3 10.6 %collective-permute-start.2 = (f32[4,16,512]{2,1,0:T(8,128)S(1)}, f32[4,16,512]{2,1,0:T(8,128)S(1)}, u32[]{:S(2)}, u32[]{:S(2)}) collective-permute-start(f32[4,16,512]{2,1,0:T(8,128)S(1)} %pad_maximum_fusion.near_ref), channel_id=1, source_target_pairs={{0,32},{16,48},{32,0},{48,16},{1,33},{17,49},{33,1},{49,17},{2,34}... | collective-permute-start | bytes 393224 | tf_op jit(solution)/shard_map/ppermute | solution.py:272

commit v6 on v5

--- a/solution.py
+++ b/solution.py
@@ -60,9 +60,8 @@
 def weigh(params, weights):
     high = weights.astype(jnp.bfloat16)
     low = (weights - high.astype(jnp.float32)).astype(jnp.bfloat16)
-    return jnp.dot(params, high, preferred_element_type=jnp.float32) + jnp.dot(
-        params, low, preferred_element_type=jnp.float32
-    )
+    twice, both = jnp.concatenate([params, params], axis=1), jnp.concatenate([high, low], axis=0)
+    return jnp.dot(twice, both, preferred_element_type=jnp.float32)
 
 
 def over_pieces(refs, step):
@@ -272,12 +271,10 @@
     return lax.ppermute(array, axis, [(i, i ^ mask) for i in range(lax.axis_size(axis))])
 
 
-def spread(array, axes):
-    order = [0]
-    for axis in axes:
-        size = lax.axis_size(axis)
-        order = [at * size + (i + size // 2) % size for at in order for i in range(size)]
-    return lax.all_to_all(array, axes, 0, 0, axis_index_groups=[order])
+def along_x(array, first):
+    count = lax.axis_size("x")
+    order = [(i + first) % count for i in range(count)]
+    return lax.all_to_all(array, "x", 0, 0, axis_index_groups=[order])
 
 
 def along_z(array, first):
@@ -290,7 +287,7 @@
     width, half = atoms.shape[1], signals.shape[1] // 2
     across, along = lax.axis_size("x"), lax.axis_size(("zh", "zl"))
     sums = project(signals, basis, across)
-    sums = spread(sums, ("x",))
+    sums = along_x(sums, 3)
     own = call(pack_kernel, shape(1, ROWS, width), atoms, params)
     near = exchange(own, "y", 1)
     sums = call(add_kernel, shape(along, PACKED, 4, half), sums)
@@ -305,7 +302,7 @@
     states = end(groups, plain, shifted, peak, sums, four, far)
     states = along_z(states, STATES_FROM)
     states = call(merge_kernel, shape(across, STATES, 2, half), states)
-    states = spread(states, ("x",))
+    states = along_x(states, 2)
     maps = call(finish_kernel, shape(3, 2 * half), states)
     return coefficients, maps
 

time: 92.8 us -> 91.6 us (0.987)
  Pallas kernels: 28.5 us -> 27.2 us
    pallas_call x1, Pallas kernels: 20.7 us -> 19.6 us  [end(): pl.pallas_call(end_kernel, out_shape=shape(2 * groups, STATES, 2, everyth...]
where the time goes in v6:
time: 91.6 us; the launch traced here: 91.1 us
  blocking collectives  36.3 us (40%)
  Pallas kernels  27.2 us (30%)
  starting transfers between devices  23.3 us (25%)
  waiting for transfers between devices  3.54 us (4%)
    all_to_all x2, blocking collectives, along_x(): return lax.all_to_all(array, 'x', 0, 0, axis_index_groups=[order])  20 us
    pallas_call x1, Pallas kernels, end(): pl.pallas_call(end_kernel, out_shape=shape(2 * groups, STATES, 2, everyth...  19.6 us
    all_to_all x1, blocking collectives, along_z(): return lax.all_to_all(array, ('zh', 'zl'), 0, 0, axis_index_groups=[order])  16.3 us
    all_to_all x1, starting transfers between devices, along_z(): return lax.all_to_all(array, ('zh', 'zl'), 0, 0, axis_index_groups=[order])  12.8 us
    ppermute x3, starting transfers between devices, exchange(): lax.ppermute(array, axis, [(i, i ^ mask) for i in range(lax.axis_size(axi...  10.5 us
    pallas_call x1, Pallas kernels, begin(): pl.pallas_call(begin_kernel, out_shape=(shape(ROWS, everything), jax.Shap...  5.29 us
    ppermute x3, waiting for transfers between devices, exchange(): lax.ppermute(array, axis, [(i, i ^ mask) for i in range(lax.axis_size(axi...  3.54 us
  transfers between devices with their start and end apart: 4, of which 2 were waited for; matrix products, arithmetic and copies ran while one was open for 0% of the time, Pallas kernels for 6%

profile of v6, /device:TPU:4, one launch (start us, length us, event | category | flops | bytes accessed | tf_op | source)
XLA Modules:
  0.0 91.1 jit_solution(13934845344906512907)
XLA Ops:
  0.6 1.0 %project.1 = f32[4,5,4,128]{3,2,1,0:T(4,128)S(1)} custom-call(bf16[125,256]{1,0:T(8,128)(2,1)} %signals_ref.1, bf16[10,125]{1,0:T(8,128)(2,1)} %basis_ref.1), custom_call_target="tpu_custom_call" | custom-call | tf_op jit(solution)/shard_map/project/pallas_call | solution.py:227
  1.6 12.1 %all_to_all.20.parts_ref = f32[4,5,4,128]{3,2,1,0:T(4,128)S(1)} all-to-all(f32[4,5,4,128]{3,2,1,0:T(4,128)S(1)} %project.1), channel_id=1, replica_groups={{384,0,128,256},{385,1,129,257},{386,2,130,258},{387,3,131,259},{388,4,..., dimensions={0} | all-to-all | bytes 81920 | tf_op jit(solution)/shard_map/all_to_all | solution.py:277
  13.8 0.7 shard_map.59
  14.4 0.0 copy-start
  14.4 0.0 copy-start.1
  14.4 12.8 %all-to-all-start.1 = ((f32[16,5,4,128]{3,2,1,0:T(4,128)}), f32[16,5,4,128]{3,2,1,0:T(4,128)S(1)}, u32[]{:S(2)}, u32[]{:S(2)}) async-start(f32[16,5,4,128]{3,2,1,0:T(4,128)} %shard_map.59), calls=%async_computation.1 | async-start | bytes 327680 | tf_op jit(solution)/shard_map/all_to_all | solution.py:283
  27.2 0.0 copy-done
  27.2 0.0 copy-done.1
  27.2 3.5 %collective-permute-start = (f32[1,16,512]{2,1,0:T(8,128)S(1)}, f32[1,16,512]{2,1,0:T(8,128)S(1)}, u32[]{:S(2)}, u32[]{:S(2)}) collective-permute-start(f32[1,16,512]{2,1,0:T(8,128)S(1)} %shard_map.60), channel_id=1, source_target_pairs={{0,16},{16,0},{32,48},{48,32},{1,17},{17,1},{33,49},{49,33},{2,18}... | collective-permute-start | bytes 98312 | tf_op jit(solution)/shard_map/ppermute | solution.py:271
  30.7 2.3 %collective-permute-done = f32[1,16,512]{2,1,0:T(8,128)S(1)} collective-permute-done((f32[1,16,512]{2,1,0:T(8,128)S(1)}, f32[1,16,512]{2,1,0:T(8,128)S(1)}, u32[]{:S(2)}, u32[]{:S(2)}) %collective-permute-start) | collective-permute-done | bytes 32800 | tf_op jit(solution)/shard_map/ppermute | solution.py:271
  33.1 1.9 %collective-permute-start.1 = (f32[2,16,512]{2,1,0:T(8,128)S(1)}, f32[2,16,512]{2,1,0:T(8,128)S(1)}, u32[]{:S(2)}, u32[]{:S(2)}) collective-permute-start(f32[2,16,512]{2,1,0:T(8,128)S(1)} %pad_maximum_fusion.1), channel_id=1, source_target_pairs={{0,1},{1,0},{2,3},{3,2},{4,5},{5,4},{6,7},{7,6},{8,9},{9,8},{10,11... | collective-permute-start | bytes 196616 | tf_op jit(solution)/shard_map/ppermute | solution.py:271
  35.0 1.2 %collective-permute-done.1 = f32[2,16,512]{2,1,0:T(8,128)S(1)} collective-permute-done((f32[2,16,512]{2,1,0:T(8,128)S(1)}, f32[2,16,512]{2,1,0:T(8,128)S(1)}, u32[]{:S(2)}, u32[]{:S(2)}) %collective-permute-start.1) | collective-permute-done | bytes 65568 | tf_op jit(solution)/shard_map/ppermute | solution.py:271
  36.2 5.1 %collective-permute-start.2 = (f32[4,16,512]{2,1,0:T(8,128)S(1)}, f32[4,16,512]{2,1,0:T(8,128)S(1)}, u32[]{:S(2)}, u32[]{:S(2)}) collective-permute-start(f32[4,16,512]{2,1,0:T(8,128)S(1)} %pad_maximum_fusion.near_ref), channel_id=1, source_target_pairs={{0,32},{16,48},{32,0},{48,16},{1,33},{17,49},{33,1},{49,17},{2,34}... | collective-permute-start | bytes 393224 | tf_op jit(solution)/shard_map/ppermute | solution.py:271
  41.3 0.0 all-to-all-done.1.coefs_ref
  41.3 5.3 %begin.1 = (f32[16,2048]{1,0:T(8,128)S(1)}, bf16[96,2048]{1,0:T(8,128)(2,1)S(1)}, f32[1,2048]{1,0:T(1,128)S(1)}, f32[16,2048]{1,0:T(8,128)S(1)}, f32[10,256]{1,0:T(8,128)}) custom-call(f32[16,5,4,128]{3,2,1,0:T(4,128)S(1)} %all-to-all-done.1.coefs_ref, f32[4,16,512]{2,1,0:T(8,128)S(1)} %pad_maximum_fusion.near_ref), custom_call_target="tpu_custom_call" | custom-call | tf_op jit(solution)/shard_map/begin/pallas_call | solution.py:159
  46.6 0.0 collective-permute-done.2.far_ref
  46.6 19.6 %end.1 = f32[16,5,2,128]{3,2,1,0:T(2,128)S(1)} custom-call(f32[16,2048]{1,0:T(8,128)S(1)} %get-tuple-element.8.plain, bf16[96,2048]{1,0:T(8,128)(2,1)S(1)} %get-tuple-element.9.shifted, f32[1,2048]{1,0:T(1,128)S(1)} %get-tuple-element.10.first_peak, f32[16,2048]{1,0:T(8,128)S(1)} %get-tuple-element.11.first_sums, ...), custom_call_target="tpu_custom_call" | custom-call | tf_op jit(solution)/shard_map/end/pallas_call | solution.py:178
  66.2 16.3 %all_to_all.21.states_ref = f32[16,5,2,128]{3,2,1,0:T(2,128)S(1)} all-to-all(f32[16,5,2,128]{3,2,1,0:T(2,128)S(1)} %end.1), channel_id=1, replica_groups={{64,66,68,70,72,74,76,78,0,2,4,6,8,10,12,14},{65,67,69,71,73,75,77,79,1..., dimensions={0} | all-to-all | bytes 163840 | tf_op jit(solution)/shard_map/all_to_all | solution.py:283
  82.5 0.1 shard_map.61
  82.6 7.9 %all_to_all.22.states_ref = f32[4,5,2,128]{3,2,1,0:T(2,128)S(1)} all-to-all(f32[4,5,2,128]{3,2,1,0:T(2,128)S(1)} %shard_map.61), channel_id=1, replica_groups={{256,384,0,128},{257,385,1,129},{258,386,2,130},{259,387,3,131},{260,38..., dimensions={0} | all-to-all | bytes 40960 | tf_op jit(solution)/shard_map/all_to_all | solution.py:277
  90.5 0.6 shard_map.62
  (3 shorter events, 0.0 us)
Async XLA Ops:
  14.4 12.8 %copy-start = (f32[10,512]{1,0:T(8,128)S(1)}, f32[10,512]{1,0:T(8,128)}, u32[]{:S(2)}) copy-start(f32[10,512]{1,0:T(8,128)} %atoms_ref.1) | copy-start | bytes 61444
  14.4 12.8 %copy-start.1 = (f32[3,512]{1,0:T(4,128)S(1)}, f32[3,512]{1,0:T(4,128)}, u32[]{:S(2)}) copy-start(f32[3,512]{1,0:T(4,128)} %params_ref.1) | copy-start | bytes 18436
  14.4 26.9 %all-to-all-start.1 = ((f32[16,5,4,128]{3,2,1,0:T(4,128)}), f32[16,5,4,128]{3,2,1,0:T(4,128)S(1)}, u32[]{:S(2)}, u32[]{:S(2)}) async-start(f32[16,5,4,128]{3,2,1,0:T(4,128)} %shard_map.59), calls=%async_computation.1 | async-start | bytes 327680 | tf_op jit(solution)/shard_map/all_to_all | solution.py:283
  27.2 5.8 %collective-permute-start = (f32[1,16,512]{2,1,0:T(8,128)S(1)}, f32[1,16,512]{2,1,0:T(8,128)S(1)}, u32[]{:S(2)}, u32[]{:S(2)}) collective-permute-start(f32[1,16,512]{2,1,0:T(8,128)S(1)} %shard_map.60), channel_id=1, source_target_pairs={{0,16},{16,0},{32,48},{48,32},{1,17},{17,1},{33,49},{49,33},{2,18}... | collective-permute-start | bytes 98312 | tf_op jit(solution)/shard_map/ppermute | solution.py:271
  33.1 3.1 %collective-permute-start.1 = (f32[2,16,512]{2,1,0:T(8,128)S(1)}, f32[2,16,512]{2,1,0:T(8,128)S(1)}, u32[]{:S(2)}, u32[]{:S(2)}) collective-permute-start(f32[2,16,512]{2,1,0:T(8,128)S(1)} %pad_maximum_fusion.1), channel_id=1, source_target_pairs={{0,1},{1,0},{2,3},{3,2},{4,5},{5,4},{6,7},{7,6},{8,9},{9,8},{10,11... | collective-permute-start | bytes 196616 | tf_op jit(solution)/shard_map/ppermute | solution.py:271
  36.2 10.4 %collective-permute-start.2 = (f32[4,16,512]{2,1,0:T(8,128)S(1)}, f32[4,16,512]{2,1,0:T(8,128)S(1)}, u32[]{:S(2)}, u32[]{:S(2)}) collective-permute-start(f32[4,16,512]{2,1,0:T(8,128)S(1)} %pad_maximum_fusion.near_ref), channel_id=1, source_target_pairs={{0,32},{16,48},{32,0},{48,16},{1,33},{17,49},{33,1},{49,17},{2,34}... | collective-permute-start | bytes 393224 | tf_op jit(solution)/shard_map/ppermute | solution.py:271

commit v7 on v6

--- a/solution.py
+++ b/solution.py
@@ -74,13 +74,20 @@
 
 
 def add_weights(pieces, shifted, sums):
-    everything = shifted.shape[1]
-    for i in range(pieces.shape[0]):
-        piece = pieces[i]
-        atoms, params = atom_terms(piece), param_terms(piece)
-        for at in range(0, everything, TILE):
-            tile = slice(at, at + TILE)
-            sums[:, tile] += weigh(params, jnp.exp2(scores_of(atoms, shifted[:, tile])))
+    everything, count = shifted.shape[1], pieces.shape[0]
+    terms = [(atom_terms(pieces[i]), param_terms(pieces[i])) for i in range(count)]
+    for at in range(0, everything, TILE):
+        tile = slice(at, at + TILE)
+        for i in range(0, count, 2):
+            left, right = [], []
+            for atoms, params in terms[i : i + 2]:
+                weights = jnp.exp2(scores_of(atoms, shifted[:, tile]))
+                high = weights.astype(jnp.bfloat16)
+                left += [params, params]
+                right += [high, (weights - high.astype(jnp.float32)).astype(jnp.bfloat16)]
+            sums[:, tile] += jnp.dot(
+                jnp.concatenate(left, axis=1), jnp.concatenate(right, axis=0), preferred_element_type=jnp.float32
+            )
 
 
 def begin_kernel(coefs_ref, near_ref, plain, shifted, peak, sums, own_coefs_ref, kept, sem):

time: 91.6 us -> 92.7 us (1.012)
  Pallas kernels: 27.2 us -> 28.4 us
where the time goes in v7:
time: 92.7 us; the launch traced here: 92.3 us
  blocking collectives  36.3 us (39%)
  Pallas kernels  28.4 us (31%)
  starting transfers between devices  23.3 us (25%)
  waiting for transfers between devices  3.54 us (4%)
    pallas_call x1, Pallas kernels, end(): pl.pallas_call(end_kernel, out_shape=shape(2 * groups, STATES, 2, everyth...  20.3 us
    all_to_all x2, blocking collectives, along_x(): return lax.all_to_all(array, 'x', 0, 0, axis_index_groups=[order])  20 us
    all_to_all x1, blocking collectives, along_z(): return lax.all_to_all(array, ('zh', 'zl'), 0, 0, axis_index_groups=[order])  16.3 us
    all_to_all x1, starting transfers between devices, along_z(): return lax.all_to_all(array, ('zh', 'zl'), 0, 0, axis_index_groups=[order])  12.8 us
    ppermute x3, starting transfers between devices, exchange(): lax.ppermute(array, axis, [(i, i ^ mask) for i in range(lax.axis_size(axi...  10.5 us
    pallas_call x1, Pallas kernels, begin(): pl.pallas_call(begin_kernel, out_shape=(shape(ROWS, everything), jax.Shap...  5.79 us
    ppermute x3, waiting for transfers between devices, exchange(): lax.ppermute(array, axis, [(i, i ^ mask) for i in range(lax.axis_size(axi...  3.54 us
  transfers between devices with their start and end apart: 4, of which 2 were waited for; matrix products, arithmetic and copies ran while one was open for 0% of the time, Pallas kernels for 6%

profile of v7, /device:TPU:4, one launch (start us, length us, event | category | flops | bytes accessed | tf_op | source)
XLA Modules:
  0.0 92.3 jit_solution(412783551141707598)
XLA Ops:
  0.6 1.0 %project.1 = f32[4,5,4,128]{3,2,1,0:T(4,128)S(1)} custom-call(bf16[125,256]{1,0:T(8,128)(2,1)} %signals_ref.1, bf16[10,125]{1,0:T(8,128)(2,1)} %basis_ref.1), custom_call_target="tpu_custom_call" | custom-call | tf_op jit(solution)/shard_map/project/pallas_call | solution.py:234
  1.6 12.1 %all_to_all.20.parts_ref = f32[4,5,4,128]{3,2,1,0:T(4,128)S(1)} all-to-all(f32[4,5,4,128]{3,2,1,0:T(4,128)S(1)} %project.1), channel_id=1, replica_groups={{384,0,128,256},{385,1,129,257},{386,2,130,258},{387,3,131,259},{388,4,..., dimensions={0} | all-to-all | bytes 81920 | tf_op jit(solution)/shard_map/all_to_all | solution.py:284
  13.8 0.7 shard_map.59
  14.4 0.0 copy-start
  14.4 0.0 copy-start.1
  14.4 12.8 %all-to-all-start.1 = ((f32[16,5,4,128]{3,2,1,0:T(4,128)}), f32[16,5,4,128]{3,2,1,0:T(4,128)S(1)}, u32[]{:S(2)}, u32[]{:S(2)}) async-start(f32[16,5,4,128]{3,2,1,0:T(4,128)} %shard_map.59), calls=%async_computation.1 | async-start | bytes 327680 | tf_op jit(solution)/shard_map/all_to_all | solution.py:290
  27.2 0.0 copy-done
  27.2 0.0 copy-done.1
  27.2 3.5 %collective-permute-start = (f32[1,16,512]{2,1,0:T(8,128)S(1)}, f32[1,16,512]{2,1,0:T(8,128)S(1)}, u32[]{:S(2)}, u32[]{:S(2)}) collective-permute-start(f32[1,16,512]{2,1,0:T(8,128)S(1)} %shard_map.60), channel_id=1, source_target_pairs={{0,16},{16,0},{32,48},{48,32},{1,17},{17,1},{33,49},{49,33},{2,18}... | collective-permute-start | bytes 98312 | tf_op jit(solution)/shard_map/ppermute | solution.py:278
  30.7 2.3 %collective-permute-done = f32[1,16,512]{2,1,0:T(8,128)S(1)} collective-permute-done((f32[1,16,512]{2,1,0:T(8,128)S(1)}, f32[1,16,512]{2,1,0:T(8,128)S(1)}, u32[]{:S(2)}, u32[]{:S(2)}) %collective-permute-start) | collective-permute-done | bytes 32800 | tf_op jit(solution)/shard_map/ppermute | solution.py:278
  33.1 1.9 %collective-permute-start.1 = (f32[2,16,512]{2,1,0:T(8,128)S(1)}, f32[2,16,512]{2,1,0:T(8,128)S(1)}, u32[]{:S(2)}, u32[]{:S(2)}) collective-permute-start(f32[2,16,512]{2,1,0:T(8,128)S(1)} %pad_maximum_fusion.1), channel_id=1, source_target_pairs={{0,1},{1,0},{2,3},{3,2},{4,5},{5,4},{6,7},{7,6},{8,9},{9,8},{10,11... | collective-permute-start | bytes 196616 | tf_op jit(solution)/shard_map/ppermute | solution.py:278
  35.0 1.2 %collective-permute-done.1 = f32[2,16,512]{2,1,0:T(8,128)S(1)} collective-permute-done((f32[2,16,512]{2,1,0:T(8,128)S(1)}, f32[2,16,512]{2,1,0:T(8,128)S(1)}, u32[]{:S(2)}, u32[]{:S(2)}) %collective-permute-start.1) | collective-permute-done | bytes 65568 | tf_op jit(solution)/shard_map/ppermute | solution.py:278
  36.2 5.1 %collective-permute-start.2 = (f32[4,16,512]{2,1,0:T(8,128)S(1)}, f32[4,16,512]{2,1,0:T(8,128)S(1)}, u32[]{:S(2)}, u32[]{:S(2)}) collective-permute-start(f32[4,16,512]{2,1,0:T(8,128)S(1)} %pad_maximum_fusion.near_ref), channel_id=1, source_target_pairs={{0,32},{16,48},{32,0},{48,16},{1,33},{17,49},{33,1},{49,17},{2,34}... | collective-permute-start | bytes 393224 | tf_op jit(solution)/shard_map/ppermute | solution.py:278
  41.3 0.0 all-to-all-done.1.coefs_ref
  41.3 5.8 %begin.1 = (f32[16,2048]{1,0:T(8,128)S(1)}, bf16[96,2048]{1,0:T(8,128)(2,1)S(1)}, f32[1,2048]{1,0:T(1,128)S(1)}, f32[16,2048]{1,0:T(8,128)S(1)}, f32[10,256]{1,0:T(8,128)}) custom-call(f32[16,5,4,128]{3,2,1,0:T(4,128)S(1)} %all-to-all-done.1.coefs_ref, f32[4,16,512]{2,1,0:T(8,128)S(1)} %pad_maximum_fusion.near_ref), custom_call_target="tpu_custom_call" | custom-call | tf_op jit(solution)/shard_map/begin/pallas_call | solution.py:166
  47.1 0.0 collective-permute-done.2.far_ref
  47.1 20.3 %end.1 = f32[16,5,2,128]{3,2,1,0:T(2,128)S(1)} custom-call(f32[16,2048]{1,0:T(8,128)S(1)} %get-tuple-element.8.plain, bf16[96,2048]{1,0:T(8,128)(2,1)S(1)} %get-tuple-element.9.shifted, f32[1,2048]{1,0:T(1,128)S(1)} %get-tuple-element.10.first_peak, f32[16,2048]{1,0:T(8,128)S(1)} %get-tuple-element.11.first_sums, ...), custom_call_target="tpu_custom_call" | custom-call | tf_op jit(solution)/shard_map/end/pallas_call | solution.py:185
  67.4 16.3 %all_to_all.21.states_ref = f32[16,5,2,128]{3,2,1,0:T(2,128)S(1)} all-to-all(f32[16,5,2,128]{3,2,1,0:T(2,128)S(1)} %end.1), channel_id=1, replica_groups={{64,66,68,70,72,74,76,78,0,2,4,6,8,10,12,14},{65,67,69,71,73,75,77,79,1..., dimensions={0} | all-to-all | bytes 163840 | tf_op jit(solution)/shard_map/all_to_all | solution.py:290
  83.7 0.1 shard_map.61
  83.7 7.9 %all_to_all.22.states_ref = f32[4,5,2,128]{3,2,1,0:T(2,128)S(1)} all-to-all(f32[4,5,2,128]{3,2,1,0:T(2,128)S(1)} %shard_map.61), channel_id=1, replica_groups={{256,384,0,128},{257,385,1,129},{258,386,2,130},{259,387,3,131},{260,38..., dimensions={0} | all-to-all | bytes 40960 | tf_op jit(solution)/shard_map/all_to_all | solution.py:284
  91.7 0.6 shard_map.62
  (3 shorter events, 0.0 us)
Async XLA Ops:
  14.4 12.8 %copy-start = (f32[10,512]{1,0:T(8,128)S(1)}, f32[10,512]{1,0:T(8,128)}, u32[]{:S(2)}) copy-start(f32[10,512]{1,0:T(8,128)} %atoms_ref.1) | copy-start | bytes 61444
  14.4 12.8 %copy-start.1 = (f32[3,512]{1,0:T(4,128)S(1)}, f32[3,512]{1,0:T(4,128)}, u32[]{:S(2)}) copy-start(f32[3,512]{1,0:T(4,128)} %params_ref.1) | copy-start | bytes 18436
  14.4 26.9 %all-to-all-start.1 = ((f32[16,5,4,128]{3,2,1,0:T(4,128)}), f32[16,5,4,128]{3,2,1,0:T(4,128)S(1)}, u32[]{:S(2)}, u32[]{:S(2)}) async-start(f32[16,5,4,128]{3,2,1,0:T(4,128)} %shard_map.59), calls=%async_computation.1 | async-start | bytes 327680 | tf_op jit(solution)/shard_map/all_to_all | solution.py:290
  27.2 5.8 %collective-permute-start = (f32[1,16,512]{2,1,0:T(8,128)S(1)}, f32[1,16,512]{2,1,0:T(8,128)S(1)}, u32[]{:S(2)}, u32[]{:S(2)}) collective-permute-start(f32[1,16,512]{2,1,0:T(8,128)S(1)} %shard_map.60), channel_id=1, source_target_pairs={{0,16},{16,0},{32,48},{48,32},{1,17},{17,1},{33,49},{49,33},{2,18}... | collective-permute-start | bytes 98312 | tf_op jit(solution)/shard_map/ppermute | solution.py:278
  33.1 3.1 %collective-permute-start.1 = (f32[2,16,512]{2,1,0:T(8,128)S(1)}, f32[2,16,512]{2,1,0:T(8,128)S(1)}, u32[]{:S(2)}, u32[]{:S(2)}) collective-permute-start(f32[2,16,512]{2,1,0:T(8,128)S(1)} %pad_maximum_fusion.1), channel_id=1, source_target_pairs={{0,1},{1,0},{2,3},{3,2},{4,5},{5,4},{6,7},{7,6},{8,9},{9,8},{10,11... | collective-permute-start | bytes 196616 | tf_op jit(solution)/shard_map/ppermute | solution.py:278
  36.2 10.9 %collective-permute-start.2 = (f32[4,16,512]{2,1,0:T(8,128)S(1)}, f32[4,16,512]{2,1,0:T(8,128)S(1)}, u32[]{:S(2)}, u32[]{:S(2)}) collective-permute-start(f32[4,16,512]{2,1,0:T(8,128)S(1)} %pad_maximum_fusion.near_ref), channel_id=1, source_target_pairs={{0,32},{16,48},{32,0},{48,16},{1,33},{17,49},{33,1},{49,17},{2,34}... | collective-permute-start | bytes 393224 | tf_op jit(solution)/shard_map/ppermute | solution.py:278
